TPU v7x, 128 devices: a whole 4x4x4 slice. The times are simulated.
128 devices in a mesh: ta: 8 (over z_hi, y), ha: 2 (over core), wa: 8 (over z_lo, x).
Axes of the slice: x: 4, y: 4, z: 4 (z_hi: 2, z_lo: 2; z = z_hi * 2 + z_lo), core: 2. Of those that a mesh axis runs over, the one named last changes fastest.
Arguments:
- queries: bfloat16 [32, 32, 64, 768], P('ta', 'ha', 'wa'), may hold values from -64 to 64
- keys: bfloat16 [32, 32, 64, 768], P('ta', 'ha', 'wa'), may hold values from -4 to 4
- values: bfloat16 [32, 32, 64, 768], P('ta', 'ha', 'wa'), may hold values from -6 to 6
- text_keys: bfloat16 [256, 768], P(('ta', 'ha', 'wa')), may hold values from -5 to 5
- text_values: bfloat16 [256, 768], P(('ta', 'ha', 'wa')), may hold values from -6 to 6
Outputs:
- attended: bfloat16 [32, 32, 64, 768], P('ta', 'ha', 'wa')
All inputs are finite; a program needn't handle non-finite values.
Results may differ from a plain program's by a relative error of at most 0.0037.
Values may be sent and summed in bfloat16 or wider, within the bound.
No kernel may reach another device: no remote copies, remote signals or barrier semaphores. Data moves between devices by JAX's collectives and lax.ppermute only.
A program may use at most 192 MiB of HBM per device.

v0:
```python
import jax
import jax.numpy as jnp
from jax import lax
from jax.sharding import PartitionSpec as P

HEADS = 6
TILE_T = 4
TILE_H = 8
TILE_W = 8


def extended(value, sides, width):
    for axis, dim in sides:
        size, length = (lax.axis_size(axis), value.shape[dim])
        up = [(i, (i + 1) % size) for i in range(size - 1)]
        down = [(j, i) for i, j in up]
        last = lax.slice_in_dim(value, length - width, length, axis=dim)
        first = lax.slice_in_dim(value, 0, width, axis=dim)
        before = lax.ppermute(last, axis, up)
        after = lax.ppermute(first, axis, down)
        value = jnp.concatenate([before, value, after], axis=dim)
    return value


def attend(query_tile, key_tile, value_tile, keep, text_keys, text_values):
    keys_all = jnp.concatenate([key_tile, text_keys], 0)
    vals_all = jnp.concatenate([value_tile, text_values], 0)
    scores = jnp.einsum(
        "qhd,khd->hqk", query_tile, keys_all, preferred_element_type=jnp.float32
    ) * query_tile.shape[2] ** (-0.5)
    allowed = jnp.concatenate([keep, jnp.ones((text_keys.shape[0],), jnp.float32) > 0.5])
    scores = jnp.where(allowed[None, None, :], scores, jnp.float32(-1e30))
    top = jnp.max(scores, -1, keepdims=True)
    weights = jnp.exp(scores - top)
    total = jnp.sum(weights, -1)
    rounded = weights.astype(jnp.bfloat16)
    summed = jnp.einsum("hqk,khd->qhd", rounded, vals_all, preferred_element_type=jnp.float32)
    return (summed / jnp.transpose(total)[:, :, None]).astype(jnp.bfloat16)


def inside_tiles(position, count, devices):
    place = position * count + jnp.arange(count + 2, dtype=jnp.int32) - 1
    return (place >= 0) & (place < count * devices)


def per_device(queries, keys, values, text_keys, text_values):
    width = queries.shape[3] // HEADS
    local_kv = jnp.stack((keys, values))
    heads_here = HEADS
    count_t = queries.shape[0] // TILE_T
    count_h = queries.shape[1] // TILE_H
    count_w = queries.shape[2] // TILE_W
    chans = queries.shape[3]
    shape7 = (count_t, TILE_T, count_h, TILE_H, count_w, TILE_W, chans)
    grid_q = queries.reshape(shape7)
    both = local_kv.reshape((2,) + shape7)
    padded = extended(both, (("ta", 1), ("ha", 3), ("wa", 5)), 1)
    keep_h = inside_tiles(lax.axis_index("ha"), count_h, lax.axis_size("ha"))
    text_pair = jnp.stack((text_keys, text_values))
    text_full = lax.all_gather(text_pair, ("ta", "ha", "wa"), axis=1, tiled=True)
    text_full = text_full.reshape(2, -1, heads_here, width)
    keep_t = inside_tiles(lax.axis_index("ta"), count_t, lax.axis_size("ta"))
    keep_w = inside_tiles(lax.axis_index("wa"), count_w, lax.axis_size("wa"))
    row_list = []
    for tile_b in range(count_h):
        window = padded[:, 0:3, :, tile_b : tile_b + 3, :, 0:3].reshape(2, -1, heads_here, width)
        mask = (
            keep_t[:, None, None, None, None, None]
            & keep_h[tile_b : tile_b + 3][None, None, :, None, None, None]
            & keep_w[None, None, None, None, :, None]
        )
        mask = jnp.broadcast_to(mask, (3, TILE_T, 3, TILE_H, 3, TILE_W)).reshape(-1)
        query_tile = grid_q[0, :, tile_b, :, 0].reshape(-1, heads_here, width)
        result = attend(query_tile, window[0], window[1], mask, text_full[0], text_full[1])
        col_list = [result.reshape(TILE_T, TILE_H, TILE_W, chans)]
        row_list.append(jnp.stack(col_list))
    plane_list = [jnp.stack(row_list)]
    tiles = jnp.stack(plane_list)
    tiles = jnp.transpose(tiles, (0, 3, 1, 4, 2, 5, 6))
    tiles = tiles.reshape(queries.shape)
    return tiles


def solution(mesh):
    placed = (
        P("ta", "ha", "wa", None),
        P("ta", "ha", "wa", None),
        P("ta", "ha", "wa", None),
        P(("ta", "ha", "wa"), None),
        P(("ta", "ha", "wa"), None),
    )
    return jax.shard_map(
        per_device, mesh=mesh, in_specs=placed, out_specs=P("ta", "ha", "wa", None), check_vma=False
    )
```

profile of v0, /device:TPU:32, one launch (start us, length us, event | category | flops | bytes accessed | tf_op | source)
XLA Modules:
  0.0 909.9 jit_solution(13567890914744605254)
XLA Ops:
  2.9 4.6 collective-permute-start
  7.6 32.1 %collective-permute-done.1 = bf16[2,1,4,2,8,1,8,768]{7,6,5,4,3,2,1,0:T(8,128)(2,1)S(1)} collective-permute-done((bf16[2,1,4,2,8,1,8,768]{7,6,5,4,3,2,1,0:T(8,128)(2,1)S(1)}, bf16[2,1,4,2,8,1,8,768]{7,6,5,4,3,2,1,0:T(8,128)(2,1)S(1)}, u32[]{:S(2)}, u32[]{:S(2)}) %collective-permute-start.1) | collective-permute-done | bytes 1572896 | tf_op jit(solution)/shard_map/ppermute | solution.py:20
  46.0 2.7 collective-permute-done.2
  48.7 2.4 collective-permute-done.3
  51.1 4.6 pad_maximum_fusion.9
  55.7 4.2 collective-permute-start.5
  63.5 510.0 %all_gather.3 = bf16[2,256,768]{2,0,1:T(2,128)(2,1)S(1)} all-gather(bf16[2,2,768]{2,0,1:T(2,128)(2,1)S(1)} %copy.51), channel_id=1, replica_groups=mesh['ta'=8,'ha'=2,'wa'=8] {'ta','ha','wa'}, dimensions={1}, use_global_device_ids=true | all-gather | bytes 792576 | tf_op jit(solution)/shard_map/all_gather | solution.py:60
  575.8 2.8 copy.52
  587.2 18.5 %pad_maximum_fusion = bf16[2,3,4,4,8,3,8,768]{7,6,5,4,3,2,1,0:T(8,128)(2,1)} fusion(bf16[2,3,4,4,8,1,8,768]{7,6,5,4,3,2,1,0:T(8,128)(2,1)} %collective-permute-done.5, bf16[2,3,4,1,8,1,8,768]{7,6,5,4,3,2,1,0:T(8,128)(2,1)} %copy-done.3, bf16[2,1,4,2,8,1,8,768]{7,6,5,4,3,2,1,0:T(8,128)(2,1)S(1)} %collective-permute-done.1, ...), kind=kLoop, calls=%fused_computation.12 | loop fusion | flops 99090432 | bytes 56623104 | tf_op jit(solution)/shard_map/concatenate | solution.py:21
  605.7 28.4 %fusion.46 = (bf16[1,3,4,3,8,3,8,768]{7,6,5,4,3,2,1,0:T(8,128)(2,1)}, bf16[1,3,4,3,8,3,8,768]{7,6,5,4,3,2,1,0:T(8,128)(2,1)}, bf16[1,3,4,3,8,3,8,768]{7,6,5,4,3,...) fusion(bf16[2,3,4,4,8,3,8,768]{7,6,5,4,3,2,1,0:T(8,128)(2,1)} %pad_maximum_fusion), kind=kLoop, calls=%fused_computation.57 | loop fusion | bytes 84934656 | tf_op jit(solution)/shard_map/slice | solution.py:74
  634.1 22.2 %squeeze.20 = bf16[6912,6,128]{2,1,0:T(8,128)(2,1)} reshape(bf16[1,3,4,3,8,3,8,768]{7,6,5,4,3,2,1,0:T(8,128)(2,1)} %get-tuple-element.5) | data formatting | bytes 21233664 | tf_op jit(solution)/shard_map/squeeze | solution.py:74
  656.4 17.3 %copy.53 = bf16[6912,6,128]{0,2,1:T(8,128)(2,1)} copy(bf16[6912,6,128]{2,1,0:T(8,128)(2,1)} %squeeze.20) | data formatting | bytes 21233664 | tf_op jit(solution)/shard_map/squeeze | solution.py:74
  673.7 22.2 %squeeze.25 = bf16[6912,6,128]{2,1,0:T(8,128)(2,1)} reshape(bf16[1,3,4,3,8,3,8,768]{7,6,5,4,3,2,1,0:T(8,128)(2,1)} %get-tuple-element.6) | data formatting | bytes 21233664 | tf_op jit(solution)/shard_map/squeeze | solution.py:74
  695.9 11.6 %copy.62 = bf16[6912,6,128]{2,0,1:T(8,128)(2,1)} copy(bf16[6912,6,128]{2,1,0:T(8,128)(2,1)} %squeeze.25) | data formatting | bytes 21233664 | tf_op jit(solution)/shard_map/squeeze | solution.py:74
  707.5 22.2 %squeeze.24 = bf16[6912,6,128]{2,1,0:T(8,128)(2,1)} reshape(bf16[1,3,4,3,8,3,8,768]{7,6,5,4,3,2,1,0:T(8,128)(2,1)} %get-tuple-element.7) | data formatting | bytes 21233664 | tf_op jit(solution)/shard_map/squeeze | solution.py:74
  729.8 17.2 %copy.61 = bf16[6912,6,128]{0,2,1:T(8,128)(2,1)} copy(bf16[6912,6,128]{2,1,0:T(8,128)(2,1)} %squeeze.24) | data formatting | bytes 21233664 | tf_op jit(solution)/shard_map/squeeze | solution.py:74
  747.0 22.2 %squeeze.22 = bf16[6912,6,128]{2,1,0:T(8,128)(2,1)} reshape(bf16[1,3,4,3,8,3,8,768]{7,6,5,4,3,2,1,0:T(8,128)(2,1)} %get-tuple-element.8) | data formatting | bytes 21233664 | tf_op jit(solution)/shard_map/squeeze | solution.py:74
  769.3 11.8 %copy.55 = bf16[6912,6,128]{2,0,1:T(8,128)(2,1)} copy(bf16[6912,6,128]{2,1,0:T(8,128)(2,1)} %squeeze.22) | data formatting | bytes 21233664 | tf_op jit(solution)/shard_map/squeeze | solution.py:74
  781.1 22.6 %bitcast_reduce_fusion.1 = (f32[6,256]{1,0:T(8,128)S(1)}, f32[6,7168,256]{2,1,0:T(8,128)}) fusion(pred[7168]{0:T(1024)(128)(4,1)S(1)} %concatenate.32, bf16[256,6,128]{2,1,0:T(8,128)(2,1)S(1)} %copy-done.5, bf16[256,6,128]{2,0,1:T(8,128)(2,1)S(1)} %copy-done.6, bf16[6912,6,128]{2,0,1:T(8,128)(2,1)} %copy.55), kind=kOutput, calls=%fused_computation.4 | convolution fusion | flops 2873620992 | bytes 55456768 | tf_op jit(solution)/shard_map/qhd,khd->hqk/dot_general | solution.py:28
  803.7 19.5 %fusion.2 = f32[6,256]{1,0:T(8,128)S(1)} fusion(f32[6,7168,256]{2,1,0:T(8,128)} %get-tuple-element.24, f32[6,256]{1,0:T(8,128)S(1)} %get-tuple-element.23, pred[7168]{0:T(1024)(128)(4,1)S(1)} %concatenate.32), kind=kLoop, calls=%fused_computation.8 | loop fusion | flops 44038656 | bytes 44059648 | tf_op jit(solution)/shard_map/reduce_sum | solution.py:35
  823.3 20.9 %fusion.33 = bf16[256,6,128]{0,2,1:T(8,128)(2,1)S(1)} fusion(f32[6,7168,256]{2,1,0:T(8,128)} %get-tuple-element.24, f32[6,256]{1,0:T(8,128)S(1)} %get-tuple-element.23, pred[7168]{0:T(1024)(128)(4,1)S(1)} %concatenate.32, bf16[256,6,128]{0,2,1:T(8,128)(2,1)S(1)} %bitcast.92, bf16[6912,6,128]{0,2,1:T(8,128)(2,1)} %copy.53, f32[256,6]{0,1:T(8,128)S(1)} %bitcast.95), kind=kOutput, calls=%fused_computation.35 | convolution fusion | flops 2885025792 | bytes 55462912 | tf_op jit(solution)/shard_map/hqk,khd->qhd/dot_general | solution.py:37
  845.0 22.7 %bitcast_reduce_fusion = (f32[6,256]{1,0:T(8,128)S(1)}, f32[6,7168,256]{2,1,0:T(8,128)}) fusion(pred[7168]{0:T(1024)(128)(4,1)S(1)} %copy-done.8, bf16[256,6,128]{2,1,0:T(8,128)(2,1)S(1)} %copy-done.4, bf16[256,6,128]{2,0,1:T(8,128)(2,1)S(1)} %copy-done.6, bf16[6912,6,128]{2,0,1:T(8,128)(2,1)} %copy.62), kind=kOutput, calls=%fused_computation.1 | convolution fusion | flops 2873620992 | bytes 55456768 | tf_op jit(solution)/shard_map/qhd,khd->hqk/dot_general | solution.py:28
  867.7 19.5 %fusion.4 = f32[6,256]{1,0:T(8,128)S(1)} fusion(f32[6,7168,256]{2,1,0:T(8,128)} %get-tuple-element.22, f32[6,256]{1,0:T(8,128)S(1)} %get-tuple-element.21, pred[7168]{0:T(1024)(128)(4,1)S(1)} %copy-done.8), kind=kLoop, calls=%fused_computation.10 | loop fusion | flops 44038656 | bytes 44059648 | tf_op jit(solution)/shard_map/reduce_sum | solution.py:35
  887.2 20.9 %fusion.27 = bf16[256,6,128]{0,2,1:T(8,128)(2,1)S(1)} fusion(f32[6,7168,256]{2,1,0:T(8,128)} %get-tuple-element.22, f32[6,256]{1,0:T(8,128)S(1)} %get-tuple-element.21, pred[7168]{0:T(1024)(128)(4,1)S(1)} %copy-done.8, bf16[256,6,128]{0,2,1:T(8,128)(2,1)S(1)} %bitcast.93, bf16[6912,6,128]{0,2,1:T(8,128)(2,1)} %copy.61, f32[256,6]{0,1:T(8,128)S(1)} %bitcast.94), kind=kOutput, calls=%fused_computation.33 | convolution fusion | flops 2885025792 | bytes 55462912 | tf_op jit(solution)/shard_map/hqk,khd->qhd/dot_general | solution.py:37
  (57 shorter events, 26.1 us)
Async XLA Ops:
  0.0 51.1 %copy-start = (bf16[4,16,8,768]{3,2,1,0:T(8,128)(2,1)S(1)}, bf16[4,16,8,768]{3,2,1,0:T(8,128)(2,1)}, u32[]{:S(2)}) copy-start(bf16[4,16,8,768]{3,2,1,0:T(8,128)(2,1)} %param.7) | copy-start | bytes 2359300
  0.0 51.1 %copy-start.1 = (bf16[4,16,8,768]{3,2,1,0:T(8,128)(2,1)S(1)}, bf16[4,16,8,768]{3,2,1,0:T(8,128)(2,1)}, u32[]{:S(2)}) copy-start(bf16[4,16,8,768]{3,2,1,0:T(8,128)(2,1)} %param.6) | copy-start | bytes 2359300
  1.6 38.0 %collective-permute-start.1 = (bf16[2,1,4,2,8,1,8,768]{7,6,5,4,3,2,1,0:T(8,128)(2,1)S(1)}, bf16[2,1,4,2,8,1,8,768]{7,6,5,4,3,2,1,0:T(8,128)(2,1)S(1)}, u32[]{:S(2)}, u32[]{:S(2)}) collective-permute-start(bf16[2,1,4,2,8,1,8,768]{7,6,5,4,3,2,1,0:T(8,128)(2,1)S(1)} %pad_maximum_fusion.11), channel_id=1, source_target_pairs={{16,0},{32,16},{48,32},{64,48},{80,64},{96,80},{112,96},{17,1},{33... | collective-permute-start | bytes 4718600 | tf_op jit(solution)/shard_map/ppermute | solution.py:20
  2.9 37.9 %collective-permute-start = (bf16[2,1,4,2,8,1,8,768]{7,6,5,4,3,2,1,0:T(8,128)(2,1)S(1)}, bf16[2,1,4,2,8,1,8,768]{7,6,5,4,3,2,1,0:T(8,128)(2,1)S(1)}, u32[]{:S(2)}, u32[]{:S(2)}) collective-permute-start(bf16[2,1,4,2,8,1,8,768]{7,6,5,4,3,2,1,0:T(8,128)(2,1)S(1)} %pad_maximum_fusion.11), channel_id=1, source_target_pairs={{0,16},{16,32},{32,48},{48,64},{64,80},{80,96},{96,112},{1,17},{17... | collective-permute-start | bytes 4718600 | tf_op jit(solution)/shard_map/ppermute | solution.py:19
  43.1 18.8 %copy-start.9 = (bf16[2,768]{1,0:T(2,128)(2,1)S(1)}, bf16[2,768]{1,0:T(2,128)(2,1)}, u32[]{:S(2)}) copy-start(bf16[2,768]{1,0:T(2,128)(2,1)} %param.9) | copy-start | bytes 9220
  43.1 18.8 %copy-start.10 = (bf16[2,768]{1,0:T(2,128)(2,1)S(1)}, bf16[2,768]{1,0:T(2,128)(2,1)}, u32[]{:S(2)}) copy-start(bf16[2,768]{1,0:T(2,128)(2,1)} %param.8) | copy-start | bytes 9220
  43.1 5.6 collective-permute-start.2
  44.7 6.4 collective-permute-start.3
  48.7 7.0 copy-start.2
  51.1 8.8 copy-start.3
  55.7 531.5 %collective-permute-start.5 = (bf16[2,3,4,4,8,1,8,768]{7,6,5,4,3,2,1,0:T(8,128)(2,1)}, bf16[2,3,4,4,8,1,8,768]{7,6,5,4,3,2,1,0:T(8,128)(2,1)}, u32[]{:S(2)}, u32[]{:S(2)}) collective-permute-start(bf16[2,3,4,4,8,1,8,768]{7,6,5,4,3,2,1,0:T(8,128)(2,1)} %pad_maximum_fusion.9), channel_id=1, source_target_pairs={{1,0},{2,1},{3,2},{4,3},{5,4},{6,5},{7,6},{9,8},{10,9},{11,10},{12... | collective-permute-start | bytes 28311560 | tf_op jit(solution)/shard_map/ppermute | solution.py:20
  59.9 527.3 %collective-permute-start.4 = (bf16[2,3,4,4,8,1,8,768]{7,6,5,4,3,2,1,0:T(8,128)(2,1)}, bf16[2,3,4,4,8,1,8,768]{7,6,5,4,3,2,1,0:T(8,128)(2,1)}, u32[]{:S(2)}, u32[]{:S(2)}) collective-permute-start(bf16[2,3,4,4,8,1,8,768]{7,6,5,4,3,2,1,0:T(8,128)(2,1)} %pad_maximum_fusion.9), channel_id=1, source_target_pairs={{0,1},{1,2},{2,3},{3,4},{4,5},{5,6},{6,7},{8,9},{9,10},{10,11},{11... | collective-permute-start | bytes 28311560 | tf_op jit(solution)/shard_map/ppermute | solution.py:19
  769.3 11.8 %copy-start.5 = (bf16[256,6,128]{2,1,0:T(8,128)(2,1)S(1)}, bf16[256,6,128]{2,1,0:T(8,128)(2,1)}, u32[]{:S(2)}) copy-start(bf16[256,6,128]{2,1,0:T(8,128)(2,1)} %reshape_squeeze.6) | copy-start | bytes 1179652
  769.3 11.8 %copy-start.6 = (bf16[256,6,128]{2,0,1:T(8,128)(2,1)S(1)}, bf16[256,6,128]{2,0,1:T(8,128)(2,1)}, u32[]{:S(2)}) copy-start(bf16[256,6,128]{2,0,1:T(8,128)(2,1)} %copy.56) | copy-start | bytes 1179652
  803.7 19.5 %copy-start.7 = (bf16[1,256,768]{1,2,0:T(8,128)(2,1)S(1)}, bf16[1,256,768]{1,2,0:T(8,128)(2,1)}, u32[]{:S(2)}) copy-start(bf16[1,256,768]{1,2,0:T(8,128)(2,1)} %copy.52) | copy-start | bytes 1179652
  823.3 21.8 %copy-start.4 = (bf16[256,6,128]{2,1,0:T(8,128)(2,1)S(1)}, bf16[256,6,128]{2,1,0:T(8,128)(2,1)}, u32[]{:S(2)}) copy-start(bf16[256,6,128]{2,1,0:T(8,128)(2,1)} %reshape_squeeze.7) | copy-start | bytes 1179652
  823.3 21.8 %copy-start.8 = (pred[7168]{0:T(1024)(128)(4,1)S(1)}, pred[7168]{0:T(1024)(128)(4,1)}, u32[]{:S(2)}) copy-start(pred[7168]{0:T(1024)(128)(4,1)} %concatenate.35) | copy-start | bytes 21508
where the time goes:
time: 923 us; the launch traced here: 910 us
  blocking collectives  510 us (55%)
  local copies, waits for them, and re-layouts  193 us (21%)
  matrix products  87.1 us (9%)
  other arithmetic  65.7 us (7%)
  waiting for transfers between devices  38.4 us (4%)
  starting transfers between devices  14.9 us (2%)
    all_gather x1, blocking collectives, per_device(): lax.all_gather(text_pair, ('ta', 'ha', 'wa'), axis=1, tiled=True)  510 us
    squeeze x4, local copies, waits for them, and re-layouts, per_device(): window[1]  79.1 us
    squeeze x4, local copies, waits for them, and re-layouts, per_device(): window[0]  67.9 us
    dot_general x2, matrix products, attend(): jnp.einsum('qhd,khd->hqk', query_tile, keys_all, preferred_element_type=j...  45.3 us
    dot_general x2, matrix products, attend(): jnp.einsum('hqk,khd->qhd', rounded, vals_all, preferred_element_type=jnp....  41.8 us
    reduce_sum x2, other arithmetic, attend(): total = jnp.sum(weights, -1)  39 us
    ppermute x3, waiting for transfers between devices, extended(): after = lax.ppermute(first, axis, down)  34.5 us
    slice x1, local copies, waits for them, and re-layouts, per_device(): window[1]  28.4 us
  transfers between devices with their start and end apart: 6, of which 4 were waited for; matrix products, arithmetic and copies ran while one was open for 2% of the time, Pallas kernels for 0%

commit v1 on v0

v1 whole, which is shorter than its diff:
```python
import functools

import jax
import jax.numpy as jnp
from jax import lax
from jax.experimental import pallas as pl
from jax.experimental.pallas import tpu as pltpu
from jax.sharding import PartitionSpec as P

HEADS = 6
TILE_T = 4
TILE_H = 8
TILE_W = 8
HD = 128
ROWS = 256
STAT_ROWS = 32
LOG2E = 1.4426950408889634
NEG = -1e30
CHUNKS = ((0, 3), (3, 5), (5, 6))
TEXT_PAD = 2


def dot_nt(a, b):
    return lax.dot_general(a, b, (((1,), (1,)), ((), ())), preferred_element_type=jnp.float32)


def split3(x):
    hi = x.astype(jnp.bfloat16).astype(jnp.float32)
    mid = (x - hi).astype(jnp.bfloat16).astype(jnp.float32)
    low = x - hi - mid
    return hi, mid, low


def attend_kernel(scale, flags, qo, ql, qr, k, v, km, kp, bo, bt, text, oo, os, ol, orr, qs, kx, vx, kbx, vbx, tx):
    bnd = flags[0]
    oks = [None, flags[1] > 0, flags[2] > 0]
    for w, ref in enumerate((qo, ql, qr)):
        for role in range(2):
            hb = bnd if role == 0 else 1 - bnd
            qs[w, role] = ref[:, hb].reshape(ROWS, HD)
    ones = jnp.ones((2 * ROWS, HD), jnp.bfloat16)
    for j, (kr, vr) in enumerate(((k, v), (km.at[0], km.at[1]), (kp.at[0], kp.at[1]))):
        kx[j] = kr[...].reshape(2 * ROWS, HD)
        vx[j, :, :HD] = vr[...].reshape(2 * ROWS, HD)
        vx[j, :, HD:] = ones
    for j, (kr, vr) in enumerate(((bo.at[0], bo.at[1]), (bt.at[0, 0], bt.at[0, 1]), (bt.at[1, 0], bt.at[1, 1]))):
        kbx[j] = kr[...].reshape(ROWS, HD)
        vbx[j, :, :HD] = vr[...].reshape(ROWS, HD)
        vbx[j, :, HD:] = ones[:ROWS]
    tx[:, :HD] = text[1]
    tx[:, HD:] = ones[:ROWS]
    mains = [(kx.at[j], vx.at[j], oks[j]) for j in range(3)]
    sides = [(kbx.at[j], vbx.at[j], oks[j]) for j in range(3)]
    texts = [(text.at[0], tx, None)]
    blocks = [(w, role, mains + (sides if role == 0 else []) + (texts if w == 0 else [])) for w in (1, 2, 0) for role in (0, 1)]
    lane = lax.broadcasted_iota(jnp.int32, (ROWS, HD), 1)
    unit = (
        lax.broadcasted_iota(jnp.int32, (16, HD), 0) == lax.broadcasted_iota(jnp.int32, (16, HD), 1)
    ).astype(jnp.float32).astype(jnp.bfloat16)

    def score(block):
        w, role, groups = block
        return [dot_nt(qs[w, role], kr[...]) for kr, _, _ in groups]

    def finish(block, scores):
        w, role, groups = block
        top = None
        for s, (_, _, ok) in zip(scores, groups):
            t = jnp.max(s, axis=1, keepdims=True)
            if ok is not None:
                t = jnp.where(ok, t, NEG)
            top = t if top is None else jnp.maximum(top, t)
        top = top * scale
        acc = None
        for s, (_, vr, ok) in zip(scores, groups):
            t = top if ok is None else jnp.where(ok, top, -NEG)
            p = jnp.exp2(s * scale - t).astype(jnp.bfloat16)
            a = jnp.dot(p, vr[...], preferred_element_type=jnp.float32)
            acc = a if acc is None else acc + a
        summed, total = acc[:, :HD], acc[:, HD:]
        hb = bnd if role == 0 else 1 - bnd
        if w == 0:
            oo[hb] = summed
            os[hb] = jnp.where(lane < 64, top, total)
            return
        out = ol if w == 1 else orr
        out[pl.ds(hb * ROWS, ROWS), :] = summed.astype(jnp.bfloat16)
        parts = jnp.zeros((ROWS, HD), jnp.float32)
        for i, part in enumerate(split3(jnp.broadcast_to(top, (ROWS, HD))) + split3(total)):
            parts = jnp.where(lane == i, part, parts)
        stats = dot_nt(unit, parts.astype(jnp.bfloat16))
        base = 2 * ROWS + 16 * hb
        out[pl.ds(base, 16), :] = jnp.concatenate([stats[:8, :HD], stats[:8, HD:]], 0).astype(jnp.bfloat16)

    held = score(blocks[0])
    for i, block in enumerate(blocks):
        ahead = score(blocks[i + 1]) if i + 1 < len(blocks) else None
        finish(block, held)
        held = ahead


def attend(flags, q, q_left, q_right, k, v, kv_minus, kv_plus, side_own, side_t, text, first, last):
    heads = last - first
    whole = lambda h: (0, 0, 0, first + h)
    part4 = pl.BlockSpec((TILE_T, 2, 64, HD), whole)
    part5 = pl.BlockSpec((2, TILE_T, 2, 64, HD), lambda h: (0, 0, 0, 0, h))
    scale = HD ** (-0.5) * LOG2E
    pairs = heads * ROWS * ROWS * 47
    sent = jax.ShapeDtypeStruct((heads, 2 * ROWS + STAT_ROWS, HD), jnp.bfloat16)
    kept = jax.ShapeDtypeStruct((heads, 2, ROWS, HD), jnp.float32)
    sent_spec = pl.BlockSpec((None, 2 * ROWS + STAT_ROWS, HD), lambda h: (h, 0, 0))
    kept_spec = pl.BlockSpec((None, 2, ROWS, HD), lambda h: (h, 0, 0, 0))
    return pl.pallas_call(
        functools.partial(attend_kernel, scale),
        grid=(heads,),
        in_specs=[
            pl.BlockSpec(memory_space=pltpu.SMEM),
            part4,
            part4,
            part4,
            part4,
            part4,
            part5,
            part5,
            pl.BlockSpec((2, TILE_T, 64, HD), whole),
            pl.BlockSpec((2, 2, TILE_T, 64, HD), lambda h: (0, 0, 0, 0, h)),
            pl.BlockSpec((2, ROWS, HD), lambda h: (0, 0, first + h)),
        ],
        out_specs=[kept_spec, kept_spec, sent_spec, sent_spec],
        out_shape=[kept, kept, sent, sent],
        scratch_shapes=[
            pltpu.VMEM((3, 2, ROWS, HD), jnp.bfloat16),
            pltpu.VMEM((3, 2 * ROWS, HD), jnp.bfloat16),
            pltpu.VMEM((3, 2 * ROWS, 2 * HD), jnp.bfloat16),
            pltpu.VMEM((3, ROWS, HD), jnp.bfloat16),
            pltpu.VMEM((3, ROWS, 2 * HD), jnp.bfloat16),
            pltpu.VMEM((ROWS, 2 * HD), jnp.bfloat16),
        ],
        compiler_params=pltpu.CompilerParams(vmem_limit_bytes=40 << 20),
        cost_estimate=pl.CostEstimate(flops=8 * HD * pairs, bytes_accessed=heads * 3000000, transcendentals=pairs),
        name=f"attend_{first}",
    )(flags, q, q_left, q_right, k, v, kv_minus, kv_plus, side_own, side_t, text)


def combine_kernel(flags, oo, os, ol, orr, *rest):
    out = rest[-1]
    eye = (
        lax.broadcasted_iota(jnp.int32, (HD, HD), 0) == lax.broadcasted_iota(jnp.int32, (HD, HD), 1)
    ).astype(jnp.float32).astype(jnp.bfloat16)
    for hb in range(2):
        tops, totals, sums = [os[hb][:, 0:1]], [os[hb][:, 64:65]], [oo[hb]]
        for ok, ref in ((flags[3] > 0, ol), (flags[4] > 0, orr)):
            base = 2 * ROWS + 16 * hb
            stats = ref[base : base + 16, :]
            cols = dot_nt(eye, stats)
            cols = jnp.concatenate([cols[:, :8], cols[:, 8:16]], 0)
            tops.append(jnp.where(ok, cols[:, 0:1] + cols[:, 1:2] + cols[:, 2:3], NEG))
            totals.append(cols[:, 3:4] + cols[:, 4:5] + cols[:, 5:6])
            sums.append(ref[hb * ROWS : (hb + 1) * ROWS, :].astype(jnp.float32))
        top = jnp.maximum(jnp.maximum(tops[0], tops[1]), tops[2])
        gains = [jnp.exp2(t - top) for t in tops]
        total = sum(g * t for g, t in zip(gains, totals))
        gains = [g / total for g in gains]
        value = sum(jnp.broadcast_to(g, (ROWS, HD)) * s for g, s in zip(gains, sums))
        out[:, hb] = value.astype(jnp.bfloat16).reshape(TILE_T, 64, HD)


def combine(flags, oo, os, o_left, o_right, before, first, last, shape):
    heads = last - first
    sent_spec = pl.BlockSpec((None, 2 * ROWS + STAT_ROWS, HD), lambda h: (h, 0, 0))
    kept_spec = pl.BlockSpec((None, 2, ROWS, HD), lambda h: (h, 0, 0, 0))
    extra = [] if before is None else [before]
    return pl.pallas_call(
        combine_kernel,
        grid=(heads,),
        in_specs=[pl.BlockSpec(memory_space=pltpu.SMEM), kept_spec, kept_spec, sent_spec, sent_spec]
        + [pl.BlockSpec(memory_space=pl.ANY)] * len(extra),
        out_specs=pl.BlockSpec((TILE_T, 2, 64, HD), lambda h: (0, 0, 0, first + h)),
        out_shape=jax.ShapeDtypeStruct(shape, jnp.bfloat16),
        input_output_aliases={5: 0} if extra else {},
        compiler_params=pltpu.CompilerParams(vmem_limit_bytes=20 << 20),
        cost_estimate=pl.CostEstimate(flops=heads * 1000000, bytes_accessed=heads * 1000000, transcendentals=0),
        name=f"combine_{first}",
    )(flags, oo, os, o_left, o_right, *extra)


def steps(axis):
    size = lax.axis_size(axis)
    up = [(i, i + 1) for i in range(size - 1)]
    return up, [(j, i) for i, j in up]


def per_device(queries, keys, values, text_keys, text_values):
    chans = queries.shape[3]
    shape = (TILE_T, 2, TILE_H * TILE_W, chans)
    q, k, v = (a.reshape(shape) for a in (queries, keys, values))
    ta, ha, wa = (lax.axis_index(a) for a in ("ta", "ha", "wa"))
    last_t, last_w = lax.axis_size("ta") - 1, lax.axis_size("wa") - 1
    side = 1 - ha
    flags = jnp.stack([side, ta > 0, ta < last_t, wa > 0, wa < last_w]).astype(jnp.int32)
    t_up, t_down = steps("ta")
    w_up, w_down = steps("wa")
    swap = [(0, 1), (1, 0)]

    rows = text_keys.shape[0]
    pad = jnp.zeros((TEXT_PAD, chans), jnp.bfloat16)
    text = lax.all_gather(jnp.concatenate([text_keys, text_values, pad], 0), ("ta", "ha", "wa"))
    text = jnp.stack([text[:, :rows].reshape(-1, chans), text[:, rows : 2 * rows].reshape(-1, chans)])

    halo = []
    for first, last in CHUNKS:
        both = jnp.stack([k[..., first * HD : last * HD], v[..., first * HD : last * HD]])
        halo.append((lax.ppermute(both, "ta", t_up), lax.ppermute(both, "ta", t_down)))
    q_left = lax.ppermute(q, "wa", w_up)
    q_right = lax.ppermute(q, "wa", w_down)
    pick = lambda a, axis: lax.dynamic_index_in_dim(a, side, axis, keepdims=False)
    side_own = lax.ppermute(jnp.stack([pick(k, 1), pick(v, 1)]), "ha", swap)

    out = None
    for (first, last), (minus, plus) in zip(CHUNKS, halo):
        side_t = lax.ppermute(jnp.stack([pick(minus, 2), pick(plus, 2)]), "ha", swap)
        oo, os, ol, orr = attend(flags, q, q_left, q_right, k, v, minus, plus, side_own, side_t, text, first, last)
        from_right = lax.ppermute(ol, "wa", w_down)
        from_left = lax.ppermute(orr, "wa", w_up)
        out = combine(flags, oo, os, from_left, from_right, out, first, last, shape)
    return out.reshape(queries.shape)


def solution(mesh):
    placed = (
        P("ta", "ha", "wa", None),
        P("ta", "ha", "wa", None),
        P("ta", "ha", "wa", None),
        P(("ta", "ha", "wa"), None),
        P(("ta", "ha", "wa"), None),
    )
    return jax.shard_map(
        per_device, mesh=mesh, in_specs=placed, out_specs=P("ta", "ha", "wa", None), check_vma=False
    )
```

time: 923 us -> 433 us (0.47); the launches traced: 910 us -> 432 us
  blocking collectives: 510 us -> 0 us
  waiting for transfers between devices: 38.4 us -> 294 us
  local copies, waits for them, and re-layouts: 193 us -> 14.7 us
  matrix products: 87.1 us -> 0 us
  other arithmetic: 65.7 us -> 8.54 us
  Pallas kernels: 0 us -> 50.6 us
  starting transfers between devices: 14.9 us -> 50.5 us
  between operations: 0.31 us -> 13.8 us
    all_gather x1 -> x0, blocking collectives: 510 us -> none  [per_device(): lax.all_gather(text_pair, ('ta', 'ha', 'wa'), axis=1, tiled=True)]
    all_gather x0 -> x1, waiting for transfers between devices: none -> 284 us  [per_device(): lax.all_gather(jnp.concatenate([text_keys, text_values, pad], 0), ('ta',...]
    squeeze x9 -> x0, local copies, waits for them, and re-layouts: 148 us -> none  [the longest x4 79.1 us: per_device(): window[1]]
    dot_general x4 -> x0, matrix products: 87.1 us -> none  [the longest x2 45.3 us: attend(): jnp.einsum('qhd,khd->hqk', query_tile, keys_all, preferred_element_type=j...]
    pallas_call x0 -> x6, Pallas kernels: none -> 50.6 us  [the longest x3 40.5 us: attend(): pl.pallas_call(functools.partial(attend_kernel, scale), grid=(heads,), in...]
    reduce_sum x2 -> x0, other arithmetic: 39 us -> none  [attend(): total = jnp.sum(weights, -1)]
    ppermute x6 -> x18, starting transfers between devices: 14.9 us -> 50.5 us  [the longest x3 18.3 us: per_device(): from_right = lax.ppermute(ol, 'wa', w_down)]
    slice x4 -> x1, local copies, waits for them, and re-layouts: 34 us -> 3.45 us  [per_device(): text[:, rows:2 * rows].reshape(-1, chans)]
  transfers between devices with their start and end apart: 6 -> 19, of which waited for: 4 -> 2; matrix products, arithmetic and copies ran while one was open for 2% -> 5% of each run, Pallas kernels for 0% -> 11%
where the time goes in v1:
time: 433 us; the launch traced here: 432 us
  waiting for transfers between devices  294 us (68%)
  Pallas kernels  50.6 us (12%)
  starting transfers between devices  50.5 us (12%)
  local copies, waits for them, and re-layouts  14.7 us (3%)
  between operations  13.8 us (3%)
  other arithmetic  8.54 us (2%)
    all_gather x1, waiting for transfers between devices, per_device(): lax.all_gather(jnp.concatenate([text_keys, text_values, pad], 0), ('ta',...  284 us
    pallas_call x3, Pallas kernels, attend(): pl.pallas_call(functools.partial(attend_kernel, scale), grid=(heads,), in...  40.5 us
    ppermute x3, starting transfers between devices, per_device(): from_right = lax.ppermute(ol, 'wa', w_down)  18.3 us
    ppermute x3, starting transfers between devices, per_device(): lax.ppermute(both, 'ta', t_up)  13.9 us
    pallas_call x3, Pallas kernels, combine(): pl.pallas_call(combine_kernel, grid=(heads,), in_specs=[pl.BlockSpec(memo...  10.1 us
    ppermute x3, waiting for transfers between devices, per_device(): lax.ppermute(both, 'ta', t_down)  9.54 us
  transfers between devices with their start and end apart: 19, of which 2 were waited for; matrix products, arithmetic and copies ran while one was open for 5% of the time, Pallas kernels for 11%

profile of v1, /device:TPU:32, one launch (start us, length us, event | category | flops | bytes accessed | tf_op | source)
XLA Modules:
  0.0 432.1 jit_solution(7284000283738715380)
XLA Ops:
  6.6 1.4 maximum_bitcast_fusion
  11.6 4.6 %collective-permute-start.13 = (bf16[2,4,2,64,384]{4,3,2,1,0:T(8,128)(2,1)}, bf16[2,4,2,64,384]{4,3,2,1,0:T(8,128)(2,1)S(1)}, u32[]{:S(2)}, u32[]{:S(2)}) collective-permute-start(bf16[2,4,2,64,384]{4,3,2,1,0:T(8,128)(2,1)} %pad_maximum_fusion.1), channel_id=1, source_target_pairs={{0,16},{16,32},{32,48},{48,64},{64,80},{80,96},{96,112},{1,17},{17... | collective-permute-start | bytes 2359304 | tf_op jit(solution)/shard_map/ppermute | solution.py:213
  18.3 5.3 %collective-permute-start.2 = (bf16[2,4,2,64,128]{4,3,2,1,0:T(8,128)(2,1)}, bf16[2,4,2,64,128]{4,3,2,1,0:T(8,128)(2,1)}, u32[]{:S(2)}, u32[]{:S(2)}) collective-permute-start(bf16[2,4,2,64,128]{4,3,2,1,0:T(8,128)(2,1)} %pad_maximum_fusion.5), channel_id=1, source_target_pairs={{0,16},{16,32},{32,48},{48,64},{64,80},{80,96},{96,112},{1,17},{17... | collective-permute-start | bytes 786440 | tf_op jit(solution)/shard_map/ppermute | solution.py:213
  26.9 2.1 pad_maximum_fusion
  28.9 9.5 %collective-permute-done.3.kp = bf16[2,4,2,64,128]{4,3,2,1,0:T(8,128)(2,1)S(1)} collective-permute-done((bf16[2,4,2,64,128]{4,3,2,1,0:T(8,128)(2,1)}, bf16[2,4,2,64,128]{4,3,2,1,0:T(8,128)(2,1)S(1)}, u32[]{:S(2)}, u32[]{:S(2)}) %collective-permute-start.3) | collective-permute-done | bytes 262176 | tf_op jit(solution)/shard_map/ppermute | solution.py:213
  38.5 4.0 collective-permute-start.8
  42.5 3.4 collective-permute-start
  47.6 4.5 %collective-permute-start.1 = (bf16[4,2,64,768]{3,2,1,0:T(8,128)(2,1)}, bf16[4,2,64,768]{3,2,1,0:T(8,128)(2,1)}, u32[]{:S(2)}, u32[]{:S(2)}) collective-permute-start(bf16[4,2,64,768]{3,2,1,0:T(8,128)(2,1)} %bitcast.5.qo), channel_id=1, source_target_pairs={{1,0},{2,1},{3,2},{4,3},{5,4},{6,5},{7,6},{9,8},{10,9},{11,10},{12... | collective-permute-start | bytes 2359304 | tf_op jit(solution)/shard_map/ppermute | solution.py:215
  56.6 284.4 %all-gather.4.cloned.1.call-done = bf16[128,6,768]{2,1,0:T(8,128)(2,1)} async-done(((bf16[1,6,768]{2,1,0:T(8,128)(2,1)}), bf16[128,6,768]{2,1,0:T(8,128)(2,1)}) %all-gather.4.cloned.1.call-update) | async-done | bytes 1179664 | tf_op jit(solution)/shard_map/all_gather | solution.py:207
  341.0 3.4 fusion
  344.4 1.9 stack_reshape.6
  346.3 1.9 stack_reshape.7
  350.5 19.7 %attend_0.1 = (f32[3,2,256,128]{3,2,1,0:T(8,128)S(1)}, f32[3,2,256,128]{3,2,1,0:T(8,128)S(1)}, bf16[3,544,128]{2,1,0:T(8,128)(2,1)S(1)}, bf16[3,544,128]{2,1,0:T(8,128)(2,1)S(1)}) custom-call(s32[5]{0:T(128)S(1)} %stack.105.flags, bf16[4,2,64,768]{3,2,1,0:T(8,128)(2,1)} %bitcast.5.qo, bf16[4,2,64,768]{3,2,1,0:T(8,128)(2,1)} %collective-permute-done.ql, ...), custom_call_target="tpu_custom_call" | custom-call | flops 9462349824 | bytes 9000000 | tf_op jit(solution)/shard_map/attend_0/pallas_call | solution.py:113
  370.2 1.9 collective-permute-start.16
  372.1 6.2 %collective-permute-start.17 = (bf16[3,544,128]{2,1,0:T(8,128)(2,1)S(1)}, bf16[3,544,128]{2,1,0:T(8,128)(2,1)S(1)}, u32[]{:S(2)}, u32[]{:S(2)}) collective-permute-start(bf16[3,544,128]{2,1,0:T(8,128)(2,1)S(1)} %get-tuple-element.28), channel_id=1, source_target_pairs={{1,0},{2,1},{3,2},{4,3},{5,4},{6,5},{7,6},{9,8},{10,9},{11,10},{12... | collective-permute-start | bytes 1253384 | tf_op jit(solution)/shard_map/ppermute | solution.py:223
  378.4 13.4 %attend_3.1 = (f32[2,2,256,128]{3,2,1,0:T(8,128)S(1)}, f32[2,2,256,128]{3,2,1,0:T(8,128)S(1)}, bf16[2,544,128]{2,1,0:T(8,128)(2,1)S(1)}, bf16[2,544,128]{2,1,0:T(8,128)(2,1)S(1)}) custom-call(s32[5]{0:T(128)S(1)} %stack.105.flags, bf16[4,2,64,768]{3,2,1,0:T(8,128)(2,1)} %bitcast.5.qo, bf16[4,2,64,768]{3,2,1,0:T(8,128)(2,1)} %collective-permute-done.ql, ...), custom_call_target="tpu_custom_call" | custom-call | flops 6308233216 | bytes 6000000 | tf_op jit(solution)/shard_map/attend_3/pallas_call | solution.py:113
  391.8 1.9 collective-permute-start.11
  393.7 6.0 %collective-permute-start.12 = (bf16[2,544,128]{2,1,0:T(8,128)(2,1)S(1)}, bf16[2,544,128]{2,1,0:T(8,128)(2,1)S(1)}, u32[]{:S(2)}, u32[]{:S(2)}) collective-permute-start(bf16[2,544,128]{2,1,0:T(8,128)(2,1)S(1)} %get-tuple-element.24), channel_id=1, source_target_pairs={{1,0},{2,1},{3,2},{4,3},{5,4},{6,5},{7,6},{9,8},{10,9},{11,10},{12... | collective-permute-start | bytes 835592 | tf_op jit(solution)/shard_map/ppermute | solution.py:223
  399.8 7.3 %attend_5.1 = (f32[1,2,256,128]{3,2,1,0:T(8,128)S(1)}, f32[1,2,256,128]{3,2,1,0:T(8,128)S(1)}, bf16[1,544,128]{2,1,0:T(8,128)(2,1)S(1)}, bf16[1,544,128]{2,1,0:T(8,128)(2,1)S(1)}) custom-call(s32[5]{0:T(128)S(1)} %stack.105.flags, bf16[4,2,64,768]{3,2,1,0:T(8,128)(2,1)} %bitcast.5.qo, bf16[4,2,64,768]{3,2,1,0:T(8,128)(2,1)} %collective-permute-done.ql, ...), custom_call_target="tpu_custom_call" | custom-call | flops 3154116608 | bytes 3000000 | tf_op jit(solution)/shard_map/attend_5/pallas_call | solution.py:113
  407.1 1.9 collective-permute-start.6
  409.0 6.0 %collective-permute-start.7 = (bf16[1,544,128]{2,1,0:T(8,128)(2,1)S(1)}, bf16[1,544,128]{2,1,0:T(8,128)(2,1)S(1)}, u32[]{:S(2)}, u32[]{:S(2)}) collective-permute-start(bf16[1,544,128]{2,1,0:T(8,128)(2,1)S(1)} %get-tuple-element.20), channel_id=1, source_target_pairs={{1,0},{2,1},{3,2},{4,3},{5,4},{6,5},{7,6},{9,8},{10,9},{11,10},{12... | collective-permute-start | bytes 417800 | tf_op jit(solution)/shard_map/ppermute | solution.py:223
  415.1 4.5 %combine_0.1.rest_0_ = bf16[4,2,64,768]{3,2,1,0:T(8,128)(2,1)} custom-call(s32[5]{0:T(128)S(1)} %stack.105.flags, f32[3,2,256,128]{3,2,1,0:T(8,128)S(1)} %get-tuple-element.25.oo, f32[3,2,256,128]{3,2,1,0:T(8,128)S(1)} %get-tuple-element.26.os, bf16[3,544,128]{2,1,0:T(8,128)(2,1)S(1)} %collective-permute-done.16.ol, ...), custom_call_target="tpu_custom_call" | custom-call | flops 3000000 | bytes 3000000 | tf_op jit(solution)/shard_map/combine_0/pallas_call | solution.py:173
  419.6 3.4 combine_3.1.rest_0_
  423.0 2.3 combine_5.1
  (57 shorter events, 17.3 us)
Async XLA Ops:
  6.5 334.4 %all-gather.4.cloned.1.call-start = ((), (), s32[]{:S(2)}) async-start(), calls=%async_computation | async-start | bytes 1585152 | tf_op jit(solution)/shard_map/all_gather | solution.py:207
  8.0 8.2 %copy-start = (bf16[4,16,8,768]{3,2,1,0:T(8,128)(2,1)S(1)}, bf16[4,16,8,768]{3,2,1,0:T(8,128)(2,1)}, u32[]{:S(2)}) copy-start(bf16[4,16,8,768]{3,2,1,0:T(8,128)(2,1)} %param.6) | copy-start | bytes 2359300
  8.0 8.2 %copy-start.1 = (bf16[4,16,8,768]{3,2,1,0:T(8,128)(2,1)S(1)}, bf16[4,16,8,768]{3,2,1,0:T(8,128)(2,1)}, u32[]{:S(2)}) copy-start(bf16[4,16,8,768]{3,2,1,0:T(8,128)(2,1)} %param.7) | copy-start | bytes 2359300
  10.3 37.3 %collective-permute-start.14 = (bf16[2,4,2,64,384]{4,3,2,1,0:T(8,128)(2,1)}, bf16[2,4,2,64,384]{4,3,2,1,0:T(8,128)(2,1)S(1)}, u32[]{:S(2)}, u32[]{:S(2)}) collective-permute-start(bf16[2,4,2,64,384]{4,3,2,1,0:T(8,128)(2,1)} %pad_maximum_fusion.1), channel_id=1, source_target_pairs={{16,0},{32,16},{48,32},{64,48},{80,64},{96,80},{112,96},{17,1},{33... | collective-permute-start | bytes 2359304 | tf_op jit(solution)/shard_map/ppermute | solution.py:213
  11.6 40.6 %collective-permute-start.13 = (bf16[2,4,2,64,384]{4,3,2,1,0:T(8,128)(2,1)}, bf16[2,4,2,64,384]{4,3,2,1,0:T(8,128)(2,1)S(1)}, u32[]{:S(2)}, u32[]{:S(2)}) collective-permute-start(bf16[2,4,2,64,384]{4,3,2,1,0:T(8,128)(2,1)} %pad_maximum_fusion.1), channel_id=1, source_target_pairs={{0,16},{16,32},{32,48},{48,64},{64,80},{80,96},{96,112},{1,17},{17... | collective-permute-start | bytes 2359304 | tf_op jit(solution)/shard_map/ppermute | solution.py:213
  17.1 21.4 %collective-permute-start.3 = (bf16[2,4,2,64,128]{4,3,2,1,0:T(8,128)(2,1)}, bf16[2,4,2,64,128]{4,3,2,1,0:T(8,128)(2,1)S(1)}, u32[]{:S(2)}, u32[]{:S(2)}) collective-permute-start(bf16[2,4,2,64,128]{4,3,2,1,0:T(8,128)(2,1)} %pad_maximum_fusion.5), channel_id=1, source_target_pairs={{16,0},{32,16},{48,32},{64,48},{80,64},{96,80},{112,96},{17,1},{33... | collective-permute-start | bytes 786440 | tf_op jit(solution)/shard_map/ppermute | solution.py:213
  18.3 24.2 %collective-permute-start.2 = (bf16[2,4,2,64,128]{4,3,2,1,0:T(8,128)(2,1)}, bf16[2,4,2,64,128]{4,3,2,1,0:T(8,128)(2,1)}, u32[]{:S(2)}, u32[]{:S(2)}) collective-permute-start(bf16[2,4,2,64,128]{4,3,2,1,0:T(8,128)(2,1)} %pad_maximum_fusion.5), channel_id=1, source_target_pairs={{0,16},{16,32},{32,48},{48,64},{64,80},{80,96},{96,112},{1,17},{17... | collective-permute-start | bytes 786440 | tf_op jit(solution)/shard_map/ppermute | solution.py:213
  24.5 28.8 %collective-permute-start.9 = (bf16[2,4,2,64,256]{4,3,2,1,0:T(8,128)(2,1)}, bf16[2,4,2,64,256]{4,3,2,1,0:T(8,128)(2,1)}, u32[]{:S(2)}, u32[]{:S(2)}) collective-permute-start(bf16[2,4,2,64,256]{4,3,2,1,0:T(8,128)(2,1)} %pad_maximum_fusion.3), channel_id=1, source_target_pairs={{16,0},{32,16},{48,32},{64,48},{80,64},{96,80},{112,96},{17,1},{33... | collective-permute-start | bytes 1572872 | tf_op jit(solution)/shard_map/ppermute | solution.py:213
  38.5 16.3 %collective-permute-start.8 = (bf16[2,4,2,64,256]{4,3,2,1,0:T(8,128)(2,1)}, bf16[2,4,2,64,256]{4,3,2,1,0:T(8,128)(2,1)S(1)}, u32[]{:S(2)}, u32[]{:S(2)}) collective-permute-start(bf16[2,4,2,64,256]{4,3,2,1,0:T(8,128)(2,1)} %pad_maximum_fusion.3), channel_id=1, source_target_pairs={{0,16},{16,32},{32,48},{48,64},{64,80},{80,96},{96,112},{1,17},{17... | collective-permute-start | bytes 1572872 | tf_op jit(solution)/shard_map/ppermute | solution.py:213
  42.5 307.9 %collective-permute-start = (bf16[4,2,64,768]{3,2,1,0:T(8,128)(2,1)}, bf16[4,2,64,768]{3,2,1,0:T(8,128)(2,1)}, u32[]{:S(2)}, u32[]{:S(2)}) collective-permute-start(bf16[4,2,64,768]{3,2,1,0:T(8,128)(2,1)} %bitcast.5.qo), channel_id=1, source_target_pairs={{0,1},{1,2},{2,3},{3,4},{4,5},{5,6},{6,7},{8,9},{9,10},{10,11},{11... | collective-permute-start | bytes 2359304 | tf_op jit(solution)/shard_map/ppermute | solution.py:214
  47.6 302.8 %collective-permute-start.1 = (bf16[4,2,64,768]{3,2,1,0:T(8,128)(2,1)}, bf16[4,2,64,768]{3,2,1,0:T(8,128)(2,1)}, u32[]{:S(2)}, u32[]{:S(2)}) collective-permute-start(bf16[4,2,64,768]{3,2,1,0:T(8,128)(2,1)} %bitcast.5.qo), channel_id=1, source_target_pairs={{1,0},{2,1},{3,2},{4,3},{5,4},{6,5},{7,6},{9,8},{10,9},{11,10},{12... | collective-permute-start | bytes 2359304 | tf_op jit(solution)/shard_map/ppermute | solution.py:215
  52.2 298.1 %collective-permute-start.4 = (bf16[2,4,64,768]{3,2,1,0:T(8,128)(2,1)}, bf16[2,4,64,768]{3,2,1,0:T(8,128)(2,1)}, u32[]{:S(2)}, u32[]{:S(2)}) collective-permute-start(bf16[2,4,64,768]{3,2,1,0:T(8,128)(2,1)} %pad_maximum_fusion), channel_id=1, source_target_pairs={{0,8},{8,0},{1,9},{9,1},{2,10},{10,2},{3,11},{11,3},{4,12},{12,4},... | collective-permute-start | bytes 2359304 | tf_op jit(solution)/shard_map/ppermute | solution.py:217
  53.3 297.1 %collective-permute-start.15 = (bf16[2,2,4,64,384]{4,3,2,1,0:T(8,128)(2,1)}, bf16[2,2,4,64,384]{4,3,2,1,0:T(8,128)(2,1)}, u32[]{:S(2)}, u32[]{:S(2)}) collective-permute-start(bf16[2,2,4,64,384]{4,3,2,1,0:T(8,128)(2,1)} %pad_maximum_fusion.2), channel_id=1, source_target_pairs={{0,8},{8,0},{1,9},{9,1},{2,10},{10,2},{3,11},{11,3},{4,12},{12,4},... | collective-permute-start | bytes 2359304 | tf_op jit(solution)/shard_map/ppermute | solution.py:221
  54.8 345.0 %collective-permute-start.5 = (bf16[2,2,4,64,128]{4,3,2,1,0:T(8,128)(2,1)}, bf16[2,2,4,64,128]{4,3,2,1,0:T(8,128)(2,1)}, u32[]{:S(2)}, u32[]{:S(2)}) collective-permute-start(bf16[2,2,4,64,128]{4,3,2,1,0:T(8,128)(2,1)} %pad_maximum_fusion.6), channel_id=1, source_target_pairs={{0,8},{8,0},{1,9},{9,1},{2,10},{10,2},{3,11},{11,3},{4,12},{12,4},... | collective-permute-start | bytes 786440 | tf_op jit(solution)/shard_map/ppermute | solution.py:221
  54.9 0.8 copy-start.2
  348.2 2.1 copy-start.4
  350.3 28.0 %copy-start.3 = (bf16[2,4,2,64,256]{4,3,2,1,0:T(8,128)(2,1)S(1)}, bf16[2,4,2,64,256]{4,3,2,1,0:T(8,128)(2,1)}, u32[]{:S(2)}) copy-start(bf16[2,4,2,64,256]{4,3,2,1,0:T(8,128)(2,1)} %copy-done.2) | copy-start | bytes 1572868
  350.3 28.0 %collective-permute-start.10 = (bf16[2,2,4,64,256]{4,3,2,1,0:T(8,128)(2,1)S(1)}, bf16[2,2,4,64,256]{4,3,2,1,0:T(8,128)(2,1)S(1)}, u32[]{:S(2)}, u32[]{:S(2)}) collective-permute-start(bf16[2,2,4,64,256]{4,3,2,1,0:T(8,128)(2,1)S(1)} %copy-done.4), channel_id=1, source_target_pairs={{0,8},{8,0},{1,9},{9,1},{2,10},{10,2},{3,11},{11,3},{4,12},{12,4},... | collective-permute-start | bytes 1572872 | tf_op jit(solution)/shard_map/ppermute | solution.py:221
  370.2 38.8 %collective-permute-start.16 = (bf16[3,544,128]{2,1,0:T(8,128)(2,1)S(1)}, bf16[3,544,128]{2,1,0:T(8,128)(2,1)S(1)}, u32[]{:S(2)}, u32[]{:S(2)}) collective-permute-start(bf16[3,544,128]{2,1,0:T(8,128)(2,1)S(1)} %get-tuple-element.27), channel_id=1, source_target_pairs={{0,1},{1,2},{2,3},{3,4},{4,5},{5,6},{6,7},{8,9},{9,10},{10,11},{11... | collective-permute-start | bytes 1253384 | tf_op jit(solution)/shard_map/ppermute | solution.py:224
  372.1 43.0 %collective-permute-start.17 = (bf16[3,544,128]{2,1,0:T(8,128)(2,1)S(1)}, bf16[3,544,128]{2,1,0:T(8,128)(2,1)S(1)}, u32[]{:S(2)}, u32[]{:S(2)}) collective-permute-start(bf16[3,544,128]{2,1,0:T(8,128)(2,1)S(1)} %get-tuple-element.28), channel_id=1, source_target_pairs={{1,0},{2,1},{3,2},{4,3},{5,4},{6,5},{7,6},{9,8},{10,9},{11,10},{12... | collective-permute-start | bytes 1253384 | tf_op jit(solution)/shard_map/ppermute | solution.py:223
  391.8 27.8 %collective-permute-start.11 = (bf16[2,544,128]{2,1,0:T(8,128)(2,1)S(1)}, bf16[2,544,128]{2,1,0:T(8,128)(2,1)S(1)}, u32[]{:S(2)}, u32[]{:S(2)}) collective-permute-start(bf16[2,544,128]{2,1,0:T(8,128)(2,1)S(1)} %get-tuple-element.23), channel_id=1, source_target_pairs={{0,1},{1,2},{2,3},{3,4},{4,5},{5,6},{6,7},{8,9},{9,10},{10,11},{11... | collective-permute-start | bytes 835592 | tf_op jit(solution)/shard_map/ppermute | solution.py:224
  393.7 25.9 %collective-permute-start.12 = (bf16[2,544,128]{2,1,0:T(8,128)(2,1)S(1)}, bf16[2,544,128]{2,1,0:T(8,128)(2,1)S(1)}, u32[]{:S(2)}, u32[]{:S(2)}) collective-permute-start(bf16[2,544,128]{2,1,0:T(8,128)(2,1)S(1)} %get-tuple-element.24), channel_id=1, source_target_pairs={{1,0},{2,1},{3,2},{4,3},{5,4},{6,5},{7,6},{9,8},{10,9},{11,10},{12... | collective-permute-start | bytes 835592 | tf_op jit(solution)/shard_map/ppermute | solution.py:223
  407.1 15.9 %collective-permute-start.6 = (bf16[1,544,128]{2,1,0:T(8,128)(2,1)S(1)}, bf16[1,544,128]{2,1,0:T(8,128)(2,1)S(1)}, u32[]{:S(2)}, u32[]{:S(2)}) collective-permute-start(bf16[1,544,128]{2,1,0:T(8,128)(2,1)S(1)} %get-tuple-element.19), channel_id=1, source_target_pairs={{0,1},{1,2},{2,3},{3,4},{4,5},{5,6},{6,7},{8,9},{9,10},{10,11},{11... | collective-permute-start | bytes 417800 | tf_op jit(solution)/shard_map/ppermute | solution.py:224
  409.0 13.9 %collective-permute-start.7 = (bf16[1,544,128]{2,1,0:T(8,128)(2,1)S(1)}, bf16[1,544,128]{2,1,0:T(8,128)(2,1)S(1)}, u32[]{:S(2)}, u32[]{:S(2)}) collective-permute-start(bf16[1,544,128]{2,1,0:T(8,128)(2,1)S(1)} %get-tuple-element.20), channel_id=1, source_target_pairs={{1,0},{2,1},{3,2},{4,3},{5,4},{6,5},{7,6},{9,8},{10,9},{11,10},{12... | collective-permute-start | bytes 417800 | tf_op jit(solution)/shard_map/ppermute | solution.py:223
Sparse Core Ops, SparseCore 0:
  9.0 331.8 all-gather.3

commit v2 on v0

v2 whole, which is shorter than its diff:
```python
import functools

import jax
import jax.numpy as jnp
from jax import lax
from jax.experimental import pallas as pl
from jax.experimental.pallas import tpu as pltpu
from jax.sharding import PartitionSpec as P

HEADS = 6
TILE_T = 4
TILE_H = 8
TILE_W = 8
HD = 128
ROWS = 256
STEP = 256
MAIN = 6 * ROWS
SIDE = 3 * ROWS
STAT_ROWS = 32
LOG2E = 1.4426950408889634
NEG = -1e30
CHUNKS = ((0, 3), (3, 6))
ALL_AXES = ("ta", "ha", "wa")


def dot_nt(a, b):
    return lax.dot_general(a, b, (((1,), (1,)), ((), ())), preferred_element_type=jnp.float32)


def unit(rows):
    row = lax.broadcasted_iota(jnp.int32, (rows, HD), 0)
    col = lax.broadcasted_iota(jnp.int32, (rows, HD), 1)
    return (row == col).astype(jnp.float32).astype(jnp.bfloat16)


def fill_keys(ks, vs, base, k, v, minus, plus, side_own, side_minus, side_plus):
    pieces = [(k[...], v[...]), (minus[0], minus[1]), (plus[0], plus[1])]
    pieces += [(s[0], s[1]) for s in (side_own, side_minus, side_plus)]
    at = base
    for kk, vv in pieces:
        rows = kk.size // HD
        ks[at : at + rows] = kk.reshape(rows, HD)
        vs[at : at + rows, :HD] = vv.reshape(rows, HD)
        at += rows
    vs[:, HD:] = jnp.ones((vs.shape[0], HD), jnp.bfloat16)


def soft_step(scale, flags, qs, ks, vs, held, text, emit):
    oks = [None, flags[1] > 0, flags[2] > 0]
    count = qs.shape[0] // STEP

    def cuts(i):
        sizes = [(text, None)] if text else []
        sizes += [(2 * ROWS, ok) for ok in oks]
        if i < count // 2:
            sizes += [(ROWS, ok) for ok in oks]
        out, at = [], 0
        for n, ok in sizes:
            out.append((at, at + n, ok))
            at += n
        return out, at

    def score(i):
        parts, n = cuts(i)
        rows = slice(i * STEP, (i + 1) * STEP)
        s = dot_nt(qs[rows], ks[:n])
        held[rows, :n] = s
        top = None
        for a, b, ok in parts:
            t = s[:, a : a + HD]
            for c in range(a + HD, b, HD):
                t = jnp.maximum(t, s[:, c : c + HD])
            if ok is not None:
                t = jnp.where(ok, t, NEG)
            top = t if top is None else jnp.maximum(top, t)
        top = jnp.max(top, axis=1, keepdims=True) * scale
        return top.astype(jnp.bfloat16).astype(jnp.float32)

    def finish(i, top):
        parts, n = cuts(i)
        rows = slice(i * STEP, (i + 1) * STEP)
        ps = []
        for a, b, ok in parts:
            t = top if ok is None else jnp.where(ok, top, -NEG)
            ps.append(jnp.exp2(held[rows, a:b] * scale - t).astype(jnp.bfloat16))
        acc = jnp.dot(jnp.concatenate(ps, 1), vs[:n], preferred_element_type=jnp.float32)
        emit(i, top, acc[:, HD:], acc[:, :HD])

    top = score(0)
    for i in range(count):
        ahead = score(i + 1) if i + 1 < count else None
        finish(i, top)
        top = ahead


def guest_kernel(scale, flags, ql, qr, k, v, minus, plus, so, sm, sp, ol, orr, ks, vs, qs, held, stats):
    head, heads = pl.program_id(0), pl.num_programs(0)
    bnd = flags[0]
    tiles = [(ref, out, hb) for hb in (bnd, 1 - bnd) for ref, out in ((ql, 0), (qr, 1))]
    for i, (ref, _, hb) in enumerate(tiles):
        qs[i * ROWS : (i + 1) * ROWS] = ref[:, hb].reshape(ROWS, HD)
    fill_keys(ks, vs, 0, k, v, minus, plus, so, sm, sp)

    @pl.when(head == 0)
    def _():
        stats[...] = jnp.zeros(stats.shape, stats.dtype)

    lane = lax.broadcasted_iota(jnp.int32, (STEP, HD), 1)
    outs = (ol, orr)

    def emit(i, top, total, summed):
        _, out, hb = tiles[i * STEP // ROWS]
        part = i * STEP % ROWS
        high = total.astype(jnp.bfloat16).astype(jnp.float32)
        outs[out][pl.ds((head * 2 + hb) * ROWS + part, STEP), :] = summed.astype(jnp.bfloat16)
        at = lane - (head * 2 + hb) * 8
        kept = jnp.where(at == 0, top, stats[out, part : part + STEP])
        kept = jnp.where(at == 1, high, kept)
        stats[out, part : part + STEP] = jnp.where(at == 2, total - high, kept)

    soft_step(scale, flags, qs, ks, vs, held, 0, emit)

    @pl.when(head == heads - 1)
    def _():
        count = ol.shape[0] // (2 * ROWS + STAT_ROWS) * 2
        for i, out in enumerate(outs):
            rows = dot_nt(unit(HD), stats[i].astype(jnp.bfloat16))
            for j in range(count):
                pair = [rows[8 * j : 8 * j + 8, :HD], rows[8 * j : 8 * j + 8, HD:]]
                at = count * ROWS + 16 * j
                out[at : at + 16, :] = jnp.concatenate(pair, 0).astype(jnp.bfloat16)


def own_kernel(scale, flags, q, k, v, minus, plus, so, sm, sp, tk, tv, ol, orr, *rest):
    out, ks, vs, qs, held, cols = rest[-6:]
    bnd, head = flags[0], pl.program_id(0)
    for i in range(2):
        qs[i * ROWS : (i + 1) * ROWS] = q[:, bnd if i == 0 else 1 - bnd].reshape(ROWS, HD)
    ks[:ROWS] = tk[...]
    vs[:ROWS, :HD] = tv[...]
    fill_keys(ks, vs, ROWS, k, v, minus, plus, so, sm, sp)

    @pl.when(head == 0)
    def _():
        count = ol.shape[0] // (2 * ROWS + STAT_ROWS) * 2
        for i, ref in enumerate((ol, orr)):
            for j in range(count):
                at = count * ROWS + 16 * j
                pair = dot_nt(unit(HD), ref[at : at + 16, :])
                cols[i, j] = jnp.concatenate([pair[:, :8], pair[:, 8:16]], 0)

    def emit(j, top, total, summed):
        hb = bnd if j * STEP < ROWS else 1 - bnd
        part = j * STEP % ROWS
        tops, totals, sums = [top], [total[:, :1]], [summed]
        for i, (ok, ref) in enumerate(((flags[3] > 0, ol), (flags[4] > 0, orr))):
            col = cols[i, head * 2 + hb, part : part + STEP]
            tops.append(jnp.where(ok, col[:, 0:1], NEG))
            totals.append(col[:, 1:2] + col[:, 2:3])
            sums.append(ref[pl.ds((head * 2 + hb) * ROWS + part, STEP), :].astype(jnp.float32))
        best = jnp.maximum(jnp.maximum(tops[0], tops[1]), tops[2])
        gains = [jnp.exp2(t - best) for t in tops]
        whole = gains[0] * totals[0] + gains[1] * totals[1] + gains[2] * totals[2]
        value = sum(jnp.broadcast_to(g / whole, (STEP, HD)) * s for g, s in zip(gains, sums))
        first = part // 64
        out[first : first + STEP // 64, hb] = value.astype(jnp.bfloat16).reshape(STEP // 64, 64, HD)

    soft_step(scale, flags, qs, ks, vs, held, ROWS, emit)


def call(kernel, name, flags, first, last, wholes, pairs5, sides5, more, more_specs, out_shape, out_specs, keys, rows, scratch, share, aliases):
    heads = last - first
    part4 = pl.BlockSpec((TILE_T, 2, 64, HD), lambda h, f: (0, 0, 0, first + h))
    part5 = pl.BlockSpec((2, TILE_T, 2, 64, HD), lambda h, f: (0, 0, 0, 0, h))
    side5 = pl.BlockSpec((2, TILE_T, None, 64, HD), lambda h, f: (0, 0, 1 - f[0], 0, h))
    pairs = heads * ROWS * ROWS * share
    return pl.pallas_call(
        functools.partial(kernel, HD ** (-0.5) * LOG2E),
        grid_spec=pltpu.PrefetchScalarGridSpec(
            num_scalar_prefetch=1,
            grid=(heads,),
            in_specs=[part4] * len(wholes) + [part5] * len(pairs5) + [side5] * len(sides5) + more_specs,
            out_specs=out_specs,
            scratch_shapes=[
                pltpu.VMEM((keys, HD), jnp.bfloat16),
                pltpu.VMEM((keys, 2 * HD), jnp.bfloat16),
                pltpu.VMEM((rows, HD), jnp.bfloat16),
                pltpu.VMEM((rows, keys), jnp.float32),
            ]
            + scratch,
        ),
        out_shape=out_shape,
        input_output_aliases=aliases,
        compiler_params=pltpu.CompilerParams(vmem_limit_bytes=56 << 20),
        cost_estimate=pl.CostEstimate(flops=8 * HD * pairs, bytes_accessed=heads * 2000000, transcendentals=pairs),
        name=f"{name}_{first}",
    )(flags, *wholes, *pairs5, *sides5, *more)


def sent_rows(first, last):
    return (last - first) * (2 * ROWS + STAT_ROWS)


def sent_spec(first, last):
    return pl.BlockSpec((sent_rows(first, last), HD), lambda h, f: (0, 0))


def guests(flags, q_left, q_right, k, v, halo, sides, first, last):
    sent = jax.ShapeDtypeStruct((sent_rows(first, last), HD), jnp.bfloat16)
    spec = sent_spec(first, last)
    scratch = [pltpu.VMEM((2, ROWS, HD), jnp.float32)]
    return call(
        guest_kernel, "guests", flags, first, last, (q_left, q_right, k, v), halo, sides, (), [],
        [sent, sent], [spec, spec], MAIN + SIDE, 4 * ROWS, scratch, 30, {},
    )


def owns(flags, q, k, v, halo, sides, text, o_left, o_right, before, first, last):
    heads = last - first
    specs = [
        pl.BlockSpec((ROWS, HD), lambda h, f: (0, first + h)),
        pl.BlockSpec((ROWS, HD), lambda h, f: (0, HEADS + first + h)),
        sent_spec(first, last),
        sent_spec(first, last),
    ]
    more = (text, text, o_left, o_right)
    aliases = {}
    if before is not None:
        more += (before,)
        specs.append(pl.BlockSpec(memory_space=pl.ANY))
        aliases = {13: 0}
    return call(
        own_kernel, "owns", flags, first, last, (q, k, v), halo, sides, more, specs,
        jax.ShapeDtypeStruct(q.shape, jnp.bfloat16),
        pl.BlockSpec((TILE_T, 2, 64, HD), lambda h, f: (0, 0, 0, first + h)),
        ROWS + MAIN + SIDE, 2 * ROWS, [pltpu.VMEM((2, 2 * heads, ROWS, 8), jnp.float32)], 17, aliases,
    )


def steps(axis):
    size = lax.axis_size(axis)
    up = [(i, i + 1) for i in range(size - 1)]
    return up, [(j, i) for i, j in up]


def per_device(queries, keys, values, text_keys, text_values):
    chans = queries.shape[3]
    shape = (TILE_T, 2, TILE_H * TILE_W, chans)
    q, k, v = (a.reshape(shape) for a in (queries, keys, values))
    ta, ha, wa = (lax.axis_index(a) for a in ALL_AXES)
    last_t, last_w = lax.axis_size("ta") - 1, lax.axis_size("wa") - 1
    flags = jnp.stack([1 - ha, ta > 0, ta < last_t, wa > 0, wa < last_w]).astype(jnp.int32)
    t_up, t_down = steps("ta")
    w_up, w_down = steps("wa")
    swap = lambda a: lax.ppermute(a, "ha", [(0, 1), (1, 0)])

    q_left = lax.ppermute(q, "wa", w_up)
    q_right = lax.ppermute(q, "wa", w_down)
    pairs = [jnp.stack([k[..., a * HD : b * HD], v[..., a * HD : b * HD]]) for a, b in CHUNKS]
    own_sides = [swap(pairs[0])]
    for i in range(1, len(pairs)):
        own_sides[-1], pairs[i] = lax.optimization_barrier((own_sides[-1], pairs[i]))
        own_sides.append(swap(pairs[i]))
    halos = [(lax.ppermute(p, "ta", t_up), lax.ppermute(p, "ta", t_down)) for p in pairs]

    count = lax.axis_size(ALL_AXES)
    text = jnp.concatenate([text_keys, text_values], 1)
    text = jnp.broadcast_to(text[None], (count,) + text.shape)
    text = lax.all_to_all(text, ALL_AXES, 0, 0, tiled=False).reshape(-1, 2 * chans)

    halos[0], text = lax.optimization_barrier((halos[0], text))
    returned, sides = [], []
    for i, ((first, last), pair) in enumerate(zip(CHUNKS, pairs)):
        halo = halos[i]
        if i > 0:
            halo, _ = halos[i], _ = lax.optimization_barrier((halo, (ol, orr)))
        sides.append((own_sides[i], swap(halo[0]), swap(halo[1])))
        ol, orr = guests(flags, q_left, q_right, k, v, halo, sides[-1], first, last)
        returned.append((lax.ppermute(orr, "wa", w_up), lax.ppermute(ol, "wa", w_down)))
    out = None
    for (first, last), halo, side, (o_left, o_right) in zip(CHUNKS, halos, sides, returned):
        out = owns(flags, q, k, v, halo, side, text, o_left, o_right, out, first, last)
    return out.reshape(queries.shape)


def solution(mesh):
    placed = (
        P("ta", "ha", "wa", None),
        P("ta", "ha", "wa", None),
        P("ta", "ha", "wa", None),
        P(("ta", "ha", "wa"), None),
        P(("ta", "ha", "wa"), None),
    )
    return jax.shard_map(
        per_device, mesh=mesh, in_specs=placed, out_specs=P("ta", "ha", "wa", None), check_vma=False
    )
```

time: 923 us -> 134 us (0.15)
  the two profiles are of different devices: /device:TPU:32 before, /device:TPU:62 now
where the time goes in v2:
time: 134 us
  Pallas kernels  43 us (32%)
  starting transfers between devices  42.6 us (32%)
  waiting for transfers between devices  37.8 us (28%)
  local copies, waits for them, and re-layouts  9.82 us (7%)
    pallas_call x4, Pallas kernels, call(): pl.pallas_call(functools.partial(kernel, HD ** (-0.5) * LOG2E), grid_spec...  43 us
    all_to_all x1, waiting for transfers between devices, per_device(): lax.all_to_all(text, ALL_AXES, 0, 0, tiled=False).reshape(-1, 2 * chans)  29.1 us
    all_to_all x1, starting transfers between devices, per_device(): lax.all_to_all(text, ALL_AXES, 0, 0, tiled=False).reshape(-1, 2 * chans)  10.4 us
    ppermute x2, starting transfers between devices, per_device(): lax.ppermute(ol, 'wa', w_down)  9.32 us
    ppermute x2, starting transfers between devices, per_device(): lax.ppermute(p, 'ta', t_up)  6.47 us
    ppermute x2, starting transfers between devices, per_device(): lax.ppermute(p, 'ta', t_down)  5.84 us
    ppermute x2, waiting for transfers between devices, per_device(): lax.ppermute(p, 'ta', t_down)  5.55 us
    ppermute x1, starting transfers between devices, per_device(): q_right = lax.ppermute(q, 'wa', w_down)  5.47 us
  transfers between devices with their start and end apart: 17, of which 3 were waited for; matrix products, arithmetic and copies ran while one was open for 2% of the time, Pallas kernels for 25%

profile of v2, /device:TPU:62, one launch (start us, length us, event | category | flops | bytes accessed | tf_op | source)
XLA Modules:
  0.0 133.6 jit_solution(14709479401881912389)
XLA Ops:
  0.0 1.5 %slice_bitcast_fusion = (bf16[1,4,2,64,384]{4,3,2,1,0:T(8,128)(2,1)S(1)}, bf16[1,4,2,64,384]{4,3,2,1,0:T(8,128)(2,1)S(1)}, bf16[1,4,2,64,384]{4,3,2,1,0:T(8,128)(2,1)S(1)}, bf16[1,4,2,64,384]{4,3,2,1,0:T(8,128)(2,1)S(1)}) fusion(bf16[4,2,64,768]{3,2,1,0:T(8,128)(2,1)} %bitcast.22, bf16[4,2,64,768]{3,2,1,0:T(8,128)(2,1)} %bitcast.17), kind=kLoop, calls=%fused_computation.2 | loop fusion | bytes 3145728 | tf_op jit(solution)/shard_map/stack | solution.py:259
  1.7 4.5 %collective-permute-start.5 = (bf16[2,4,2,64,384]{4,3,2,1,0:T(8,128)(2,1)S(1)}, bf16[2,4,2,64,384]{4,3,2,1,0:T(8,128)(2,1)}, u32[]{:S(2)}, u32[]{:S(2)}) collective-permute-start(bf16[2,4,2,64,384]{4,3,2,1,0:T(8,128)(2,1)S(1)} %pad_maximum_fusion), channel_id=1, source_target_pairs={{0,16},{16,32},{32,48},{48,64},{64,80},{80,96},{96,112},{1,17},{17... | collective-permute-start | bytes 2359304 | tf_op jit(solution)/shard_map/ppermute | solution.py:264
  6.2 1.9 %collective-permute-start.6 = (bf16[2,4,2,64,384]{4,3,2,1,0:T(8,128)(2,1)S(1)}, bf16[2,4,2,64,384]{4,3,2,1,0:T(8,128)(2,1)}, u32[]{:S(2)}, u32[]{:S(2)}) collective-permute-start(bf16[2,4,2,64,384]{4,3,2,1,0:T(8,128)(2,1)S(1)} %pad_maximum_fusion), channel_id=1, source_target_pairs={{16,0},{32,16},{48,32},{64,48},{80,64},{96,80},{112,96},{17,1},{33... | collective-permute-start | bytes 2359304 | tf_op jit(solution)/shard_map/ppermute | solution.py:264
  8.2 1.3 broadcast_in_dim.2
  9.5 10.4 %all-to-all-start = ((bf16[128,2,1536]{2,1,0:T(2,128)(2,1)}), bf16[128,2,1536]{2,1,0:T(2,128)(2,1)S(1)}, u32[]{:S(2)}, u32[]{:S(2)}) async-start(bf16[128,2,1536]{2,1,0:T(2,128)(2,1)} %broadcast_in_dim.2), calls=%async_computation | async-start | bytes 1572864 | tf_op jit(solution)/shard_map/all_to_all | solution.py:269
  20.1 1.3 collective-permute-start.3
  21.4 5.5 %collective-permute-start.4 = (bf16[4,2,64,768]{3,2,1,0:T(8,128)(2,1)S(1)}, bf16[4,2,64,768]{3,2,1,0:T(8,128)(2,1)}, u32[]{:S(2)}, u32[]{:S(2)}) collective-permute-start(bf16[4,2,64,768]{3,2,1,0:T(8,128)(2,1)S(1)} %bitcast.30), channel_id=1, source_target_pairs={{1,0},{2,1},{3,2},{4,3},{5,4},{6,5},{7,6},{9,8},{10,9},{11,10},{12... | collective-permute-start | bytes 2359304 | tf_op jit(solution)/shard_map/ppermute | solution.py:258
  26.9 29.1 %all-to-all-done = bf16[128,2,1536]{2,1,0:T(2,128)(2,1)S(1)} async-done(((bf16[128,2,1536]{2,1,0:T(2,128)(2,1)}), bf16[128,2,1536]{2,1,0:T(2,128)(2,1)S(1)}, u32[]{:S(2)}, u32[]{:S(2)}) %all-to-all-start) | async-done | bytes 786464 | tf_op jit(solution)/shard_map/all_to_all | solution.py:269
  56.0 1.2 reshape.19.tk.tv
  57.8 1.9 %collective-permute-start.1 = (bf16[2,4,2,64,384]{4,3,2,1,0:T(8,128)(2,1)S(1)}, bf16[2,4,2,64,384]{4,3,2,1,0:T(8,128)(2,1)S(1)}, u32[]{:S(2)}, u32[]{:S(2)}) collective-permute-start(bf16[2,4,2,64,384]{4,3,2,1,0:T(8,128)(2,1)S(1)} %pad_maximum_fusion.1), channel_id=1, source_target_pairs={{0,16},{16,32},{32,48},{48,64},{64,80},{80,96},{96,112},{1,17},{17... | collective-permute-start | bytes 2359304 | tf_op jit(solution)/shard_map/ppermute | solution.py:264
  59.8 3.9 %collective-permute-start.2 = (bf16[2,4,2,64,384]{4,3,2,1,0:T(8,128)(2,1)S(1)}, bf16[2,4,2,64,384]{4,3,2,1,0:T(8,128)(2,1)S(1)}, u32[]{:S(2)}, u32[]{:S(2)}) collective-permute-start(bf16[2,4,2,64,384]{4,3,2,1,0:T(8,128)(2,1)S(1)} %pad_maximum_fusion.1), channel_id=1, source_target_pairs={{16,0},{32,16},{48,32},{64,48},{80,64},{96,80},{112,96},{17,1},{33... | collective-permute-start | bytes 2359304 | tf_op jit(solution)/shard_map/ppermute | solution.py:264
  64.4 11.8 %guests_0.1 = (bf16[1632,128]{1,0:T(8,128)(2,1)}, bf16[1632,128]{1,0:T(8,128)(2,1)}) custom-call(s32[5]{0:T(128)} %stack.57.flags, bf16[4,2,64,768]{3,2,1,0:T(8,128)(2,1)} %collective-permute-done.3.ql, bf16[4,2,64,768]{3,2,1,0:T(8,128)(2,1)} %collective-permute-done.4.qr, bf16[4,2,64,768]{3,2,1,0:T(8,128)(2,1)} %bitcast.18, ...), custom_call_target="tpu_custom_call" | custom-call | flops 6039797760 | bytes 6000000 | tf_op jit(solution)/shard_map/guests_0/pallas_call | solution.py:177
  76.2 3.0 %collective-permute-done.1.minus = bf16[2,4,2,64,384]{4,3,2,1,0:T(8,128)(2,1)S(1)} collective-permute-done((bf16[2,4,2,64,384]{4,3,2,1,0:T(8,128)(2,1)S(1)}, bf16[2,4,2,64,384]{4,3,2,1,0:T(8,128)(2,1)S(1)}, u32[]{:S(2)}, u32[]{:S(2)}) %collective-permute-start.1) | collective-permute-done | bytes 786464 | tf_op jit(solution)/shard_map/ppermute | solution.py:264
  79.3 5.5 %collective-permute-done.2.plus = bf16[2,4,2,64,384]{4,3,2,1,0:T(8,128)(2,1)S(1)} collective-permute-done((bf16[2,4,2,64,384]{4,3,2,1,0:T(8,128)(2,1)S(1)}, bf16[2,4,2,64,384]{4,3,2,1,0:T(8,128)(2,1)S(1)}, u32[]{:S(2)}, u32[]{:S(2)}) %collective-permute-start.2) | collective-permute-done | bytes 786464 | tf_op jit(solution)/shard_map/ppermute | solution.py:264
  85.3 1.3 collective-permute-start.14
  86.6 4.6 %collective-permute-start.15 = (bf16[1632,128]{1,0:T(8,128)(2,1)}, bf16[1632,128]{1,0:T(8,128)(2,1)S(1)}, u32[]{:S(2)}, u32[]{:S(2)}) collective-permute-start(bf16[1632,128]{1,0:T(8,128)(2,1)} %get-tuple-element.20), channel_id=1, source_target_pairs={{1,0},{2,1},{3,2},{4,3},{5,4},{6,5},{7,6},{9,8},{10,9},{11,10},{12... | collective-permute-start | bytes 1253384 | tf_op jit(solution)/shard_map/ppermute | solution.py:279
  91.3 0.8 copy-done.5
  92.4 0.9 copy-done.7
  93.3 11.8 %guests_3.1 = (bf16[1632,128]{1,0:T(8,128)(2,1)}, bf16[1632,128]{1,0:T(8,128)(2,1)}) custom-call(s32[5]{0:T(128)} %stack.57.flags, bf16[4,2,64,768]{3,2,1,0:T(8,128)(2,1)} %collective-permute-done.3.ql, bf16[4,2,64,768]{3,2,1,0:T(8,128)(2,1)} %collective-permute-done.4.qr, bf16[4,2,64,768]{3,2,1,0:T(8,128)(2,1)} %bitcast.19, ...), custom_call_target="tpu_custom_call" | custom-call | flops 6039797760 | bytes 6000000 | tf_op jit(solution)/shard_map/guests_3/pallas_call | solution.py:177
  105.1 1.3 collective-permute-start.12
  106.4 4.8 %collective-permute-start.13 = (bf16[1632,128]{1,0:T(8,128)(2,1)}, bf16[1632,128]{1,0:T(8,128)(2,1)S(1)}, u32[]{:S(2)}, u32[]{:S(2)}) collective-permute-start(bf16[1632,128]{1,0:T(8,128)(2,1)} %get-tuple-element.26), channel_id=1, source_target_pairs={{1,0},{2,1},{3,2},{4,3},{5,4},{6,5},{7,6},{9,8},{10,9},{11,10},{12... | collective-permute-start | bytes 1253384 | tf_op jit(solution)/shard_map/ppermute | solution.py:279
  112.8 9.6 %owns_0.1.rest_0_ = bf16[4,2,64,768]{3,2,1,0:T(8,128)(2,1)} custom-call(s32[5]{0:T(128)} %stack.57.flags, bf16[4,2,64,768]{3,2,1,0:T(8,128)(2,1)} %bitcast.27, bf16[4,2,64,768]{3,2,1,0:T(8,128)(2,1)} %bitcast.20, bf16[4,2,64,768]{3,2,1,0:T(8,128)(2,1)} %bitcast.25, bf16[2,4,2,64,384]{4,3,2,1,0:T(8,128)(2,1)} %collective-permute-done.5.minus, ...), custom_call_target="tpu_custom_call" | custom-call | flops 3422552064 | bytes 6000000 | tf_op jit(solution)/shard_map/owns_0/pallas_call | solution.py:177
  122.4 0.8 copy-done.10
  124.0 9.7 %owns_3.1 = bf16[4,2,64,768]{3,2,1,0:T(8,128)(2,1)} custom-call(s32[5]{0:T(128)} %stack.57.flags, bf16[4,2,64,768]{3,2,1,0:T(8,128)(2,1)} %bitcast.28, bf16[4,2,64,768]{3,2,1,0:T(8,128)(2,1)} %bitcast.21, bf16[4,2,64,768]{3,2,1,0:T(8,128)(2,1)} %bitcast.26, bf16[2,4,2,64,384]{4,3,2,1,0:T(8,128)(2,1)} %copy-done.3, ...), custom_call_target="tpu_custom_call", output_to_operand_aliasing={{}: (13, {})} | custom-call | flops 3422552064 | bytes 6000000 | tf_op jit(solution)/shard_map/owns_3/pallas_call | solution.py:177
  (45 shorter events, 4.7 us)
Async XLA Ops:
  1.6 6.6 %copy-start = (bf16[2,768]{1,0:T(2,128)(2,1)S(1)}, bf16[2,768]{1,0:T(2,128)(2,1)}, u32[]{:S(2)}) copy-start(bf16[2,768]{1,0:T(2,128)(2,1)} %param.9) | copy-start | bytes 9220
  1.6 6.6 %copy-start.1 = (bf16[2,768]{1,0:T(2,128)(2,1)S(1)}, bf16[2,768]{1,0:T(2,128)(2,1)}, u32[]{:S(2)}) copy-start(bf16[2,768]{1,0:T(2,128)(2,1)} %param.8) | copy-start | bytes 9220
  1.7 55.5 %collective-permute-start.5 = (bf16[2,4,2,64,384]{4,3,2,1,0:T(8,128)(2,1)S(1)}, bf16[2,4,2,64,384]{4,3,2,1,0:T(8,128)(2,1)}, u32[]{:S(2)}, u32[]{:S(2)}) collective-permute-start(bf16[2,4,2,64,384]{4,3,2,1,0:T(8,128)(2,1)S(1)} %pad_maximum_fusion), channel_id=1, source_target_pairs={{0,16},{16,32},{32,48},{48,64},{64,80},{80,96},{96,112},{1,17},{17... | collective-permute-start | bytes 2359304 | tf_op jit(solution)/shard_map/ppermute | solution.py:264
  6.2 51.0 %collective-permute-start.6 = (bf16[2,4,2,64,384]{4,3,2,1,0:T(8,128)(2,1)S(1)}, bf16[2,4,2,64,384]{4,3,2,1,0:T(8,128)(2,1)}, u32[]{:S(2)}, u32[]{:S(2)}) collective-permute-start(bf16[2,4,2,64,384]{4,3,2,1,0:T(8,128)(2,1)S(1)} %pad_maximum_fusion), channel_id=1, source_target_pairs={{16,0},{32,16},{48,32},{64,48},{80,64},{96,80},{112,96},{17,1},{33... | collective-permute-start | bytes 2359304 | tf_op jit(solution)/shard_map/ppermute | solution.py:264
  9.5 10.7 %copy-start.2 = (bf16[4,16,8,768]{3,2,1,0:T(8,128)(2,1)S(1)}, bf16[4,16,8,768]{3,2,1,0:T(8,128)(2,1)}, u32[]{:S(2)}) copy-start(bf16[4,16,8,768]{3,2,1,0:T(8,128)(2,1)} %param.5) | copy-start | bytes 2359300
  9.5 46.5 %all-to-all-start = ((bf16[128,2,1536]{2,1,0:T(2,128)(2,1)}), bf16[128,2,1536]{2,1,0:T(2,128)(2,1)S(1)}, u32[]{:S(2)}, u32[]{:S(2)}) async-start(bf16[128,2,1536]{2,1,0:T(2,128)(2,1)} %broadcast_in_dim.2), calls=%async_computation | async-start | bytes 1572864 | tf_op jit(solution)/shard_map/all_to_all | solution.py:269
  19.9 37.9 %collective-permute-start = (bf16[2,4,2,64,384]{4,3,2,1,0:T(8,128)(2,1)S(1)}, bf16[2,4,2,64,384]{4,3,2,1,0:T(8,128)(2,1)}, u32[]{:S(2)}, u32[]{:S(2)}) collective-permute-start(bf16[2,4,2,64,384]{4,3,2,1,0:T(8,128)(2,1)S(1)} %pad_maximum_fusion), channel_id=1, source_target_pairs={{0,8},{8,0},{1,9},{9,1},{2,10},{10,2},{3,11},{11,3},{4,12},{12,4},... | collective-permute-start | bytes 2359304 | tf_op jit(solution)/shard_map/ppermute | solution.py:255
  20.1 39.6 %collective-permute-start.3 = (bf16[4,2,64,768]{3,2,1,0:T(8,128)(2,1)S(1)}, bf16[4,2,64,768]{3,2,1,0:T(8,128)(2,1)}, u32[]{:S(2)}, u32[]{:S(2)}) collective-permute-start(bf16[4,2,64,768]{3,2,1,0:T(8,128)(2,1)S(1)} %bitcast.29), channel_id=1, source_target_pairs={{0,1},{1,2},{2,3},{3,4},{4,5},{5,6},{6,7},{8,9},{9,10},{10,11},{11... | collective-permute-start | bytes 2359304 | tf_op jit(solution)/shard_map/ppermute | solution.py:257
  21.4 43.0 %collective-permute-start.4 = (bf16[4,2,64,768]{3,2,1,0:T(8,128)(2,1)S(1)}, bf16[4,2,64,768]{3,2,1,0:T(8,128)(2,1)}, u32[]{:S(2)}, u32[]{:S(2)}) collective-permute-start(bf16[4,2,64,768]{3,2,1,0:T(8,128)(2,1)S(1)} %bitcast.30), channel_id=1, source_target_pairs={{1,0},{2,1},{3,2},{4,3},{5,4},{6,5},{7,6},{9,8},{10,9},{11,10},{12... | collective-permute-start | bytes 2359304 | tf_op jit(solution)/shard_map/ppermute | solution.py:258
  57.2 7.2 %collective-permute-start.7 = (bf16[2,4,2,64,384]{4,3,2,1,0:T(8,128)(2,1)}, bf16[2,4,2,64,384]{4,3,2,1,0:T(8,128)(2,1)}, u32[]{:S(2)}, u32[]{:S(2)}) collective-permute-start(bf16[2,4,2,64,384]{4,3,2,1,0:T(8,128)(2,1)} %collective-permute-done.5.minus), channel_id=1, source_target_pairs={{0,8},{8,0},{1,9},{9,1},{2,10},{10,2},{3,11},{11,3},{4,12},{12,4},... | collective-permute-start | bytes 2359304 | tf_op jit(solution)/shard_map/ppermute | solution.py:255
  57.2 7.2 %collective-permute-start.8 = (bf16[2,4,2,64,384]{4,3,2,1,0:T(8,128)(2,1)}, bf16[2,4,2,64,384]{4,3,2,1,0:T(8,128)(2,1)}, u32[]{:S(2)}, u32[]{:S(2)}) collective-permute-start(bf16[2,4,2,64,384]{4,3,2,1,0:T(8,128)(2,1)} %collective-permute-done.6.plus), channel_id=1, source_target_pairs={{0,8},{8,0},{1,9},{9,1},{2,10},{10,2},{3,11},{11,3},{4,12},{12,4},... | collective-permute-start | bytes 2359304 | tf_op jit(solution)/shard_map/ppermute | solution.py:255
  57.8 21.4 %collective-permute-start.1 = (bf16[2,4,2,64,384]{4,3,2,1,0:T(8,128)(2,1)S(1)}, bf16[2,4,2,64,384]{4,3,2,1,0:T(8,128)(2,1)S(1)}, u32[]{:S(2)}, u32[]{:S(2)}) collective-permute-start(bf16[2,4,2,64,384]{4,3,2,1,0:T(8,128)(2,1)S(1)} %pad_maximum_fusion.1), channel_id=1, source_target_pairs={{0,16},{16,32},{32,48},{48,64},{64,80},{80,96},{96,112},{1,17},{17... | collective-permute-start | bytes 2359304 | tf_op jit(solution)/shard_map/ppermute | solution.py:264
  59.8 25.0 %collective-permute-start.2 = (bf16[2,4,2,64,384]{4,3,2,1,0:T(8,128)(2,1)S(1)}, bf16[2,4,2,64,384]{4,3,2,1,0:T(8,128)(2,1)S(1)}, u32[]{:S(2)}, u32[]{:S(2)}) collective-permute-start(bf16[2,4,2,64,384]{4,3,2,1,0:T(8,128)(2,1)S(1)} %pad_maximum_fusion.1), channel_id=1, source_target_pairs={{16,0},{32,16},{48,32},{64,48},{80,64},{96,80},{112,96},{17,1},{33... | collective-permute-start | bytes 2359304 | tf_op jit(solution)/shard_map/ppermute | solution.py:264
  64.4 26.8 %collective-permute-start.9 = (bf16[2,4,2,64,384]{4,3,2,1,0:T(8,128)(2,1)S(1)}, bf16[2,4,2,64,384]{4,3,2,1,0:T(8,128)(2,1)S(1)}, u32[]{:S(2)}, u32[]{:S(2)}) collective-permute-start(bf16[2,4,2,64,384]{4,3,2,1,0:T(8,128)(2,1)S(1)} %pad_maximum_fusion.1), channel_id=1, source_target_pairs={{0,8},{8,0},{1,9},{9,1},{2,10},{10,2},{3,11},{11,3},{4,12},{12,4},... | collective-permute-start | bytes 2359304 | tf_op jit(solution)/shard_map/ppermute | solution.py:255
  79.3 12.0 %copy-start.3 = (bf16[2,4,2,64,384]{4,3,2,1,0:T(8,128)(2,1)}, bf16[2,4,2,64,384]{4,3,2,1,0:T(8,128)(2,1)S(1)}, u32[]{:S(2)}) copy-start(bf16[2,4,2,64,384]{4,3,2,1,0:T(8,128)(2,1)S(1)} %collective-permute-done.1.minus) | copy-start | bytes 2359300
  84.8 6.4 %copy-start.4 = (bf16[2,4,2,64,384]{4,3,2,1,0:T(8,128)(2,1)}, bf16[2,4,2,64,384]{4,3,2,1,0:T(8,128)(2,1)S(1)}, u32[]{:S(2)}) copy-start(bf16[2,4,2,64,384]{4,3,2,1,0:T(8,128)(2,1)S(1)} %collective-permute-done.2.plus) | copy-start | bytes 2359300
  84.8 6.4 %collective-permute-start.10 = (bf16[2,4,2,64,384]{4,3,2,1,0:T(8,128)(2,1)S(1)}, bf16[2,4,2,64,384]{4,3,2,1,0:T(8,128)(2,1)S(1)}, u32[]{:S(2)}, u32[]{:S(2)}) collective-permute-start(bf16[2,4,2,64,384]{4,3,2,1,0:T(8,128)(2,1)S(1)} %collective-permute-done.1.minus), channel_id=1, source_target_pairs={{0,8},{8,0},{1,9},{9,1},{2,10},{10,2},{3,11},{11,3},{4,12},{12,4},... | collective-permute-start | bytes 2359304 | tf_op jit(solution)/shard_map/ppermute | solution.py:255
  84.8 6.4 %collective-permute-start.11 = (bf16[2,4,2,64,384]{4,3,2,1,0:T(8,128)(2,1)S(1)}, bf16[2,4,2,64,384]{4,3,2,1,0:T(8,128)(2,1)S(1)}, u32[]{:S(2)}, u32[]{:S(2)}) collective-permute-start(bf16[2,4,2,64,384]{4,3,2,1,0:T(8,128)(2,1)S(1)} %collective-permute-done.2.plus), channel_id=1, source_target_pairs={{0,8},{8,0},{1,9},{9,1},{2,10},{10,2},{3,11},{11,3},{4,12},{12,4},... | collective-permute-start | bytes 2359304 | tf_op jit(solution)/shard_map/ppermute | solution.py:255
  85.3 25.9 %collective-permute-start.14 = (bf16[1632,128]{1,0:T(8,128)(2,1)}, bf16[1632,128]{1,0:T(8,128)(2,1)S(1)}, u32[]{:S(2)}, u32[]{:S(2)}) collective-permute-start(bf16[1632,128]{1,0:T(8,128)(2,1)} %get-tuple-element.21), channel_id=1, source_target_pairs={{0,1},{1,2},{2,3},{3,4},{4,5},{5,6},{6,7},{8,9},{9,10},{10,11},{11... | collective-permute-start | bytes 1253384 | tf_op jit(solution)/shard_map/ppermute | solution.py:279
  86.6 24.6 %collective-permute-start.15 = (bf16[1632,128]{1,0:T(8,128)(2,1)}, bf16[1632,128]{1,0:T(8,128)(2,1)S(1)}, u32[]{:S(2)}, u32[]{:S(2)}) collective-permute-start(bf16[1632,128]{1,0:T(8,128)(2,1)} %get-tuple-element.20), channel_id=1, source_target_pairs={{1,0},{2,1},{3,2},{4,3},{5,4},{6,5},{7,6},{9,8},{10,9},{11,10},{12... | collective-permute-start | bytes 1253384 | tf_op jit(solution)/shard_map/ppermute | solution.py:279
  91.2 1.1 copy-start.6
  92.4 0.9 copy-start.7
  105.1 17.3 %collective-permute-start.12 = (bf16[1632,128]{1,0:T(8,128)(2,1)}, bf16[1632,128]{1,0:T(8,128)(2,1)S(1)}, u32[]{:S(2)}, u32[]{:S(2)}) collective-permute-start(bf16[1632,128]{1,0:T(8,128)(2,1)} %get-tuple-element.25), channel_id=1, source_target_pairs={{0,1},{1,2},{2,3},{3,4},{4,5},{5,6},{6,7},{8,9},{9,10},{10,11},{11... | collective-permute-start | bytes 1253384 | tf_op jit(solution)/shard_map/ppermute | solution.py:279
  106.4 16.0 %collective-permute-start.13 = (bf16[1632,128]{1,0:T(8,128)(2,1)}, bf16[1632,128]{1,0:T(8,128)(2,1)S(1)}, u32[]{:S(2)}, u32[]{:S(2)}) collective-permute-start(bf16[1632,128]{1,0:T(8,128)(2,1)} %get-tuple-element.26), channel_id=1, source_target_pairs={{1,0},{2,1},{3,2},{4,3},{5,4},{6,5},{7,6},{9,8},{10,9},{11,10},{12... | collective-permute-start | bytes 1253384 | tf_op jit(solution)/shard_map/ppermute | solution.py:279
  (5 other events, 4.0 us)

commit v3 on v2

--- a/solution.py
+++ b/solution.py
@@ -45,7 +45,7 @@
     vs[:, HD:] = jnp.ones((vs.shape[0], HD), jnp.bfloat16)
 
 
-def soft_step(scale, flags, qs, ks, vs, held, text, emit):
+def soft_step(scale, flags, qs, ks, vs, held, text, emit, exact):
     oks = [None, flags[1] > 0, flags[2] > 0]
     count = qs.shape[0] // STEP
 
@@ -74,7 +74,7 @@
                 t = jnp.where(ok, t, NEG)
             top = t if top is None else jnp.maximum(top, t)
         top = jnp.max(top, axis=1, keepdims=True) * scale
-        return top.astype(jnp.bfloat16).astype(jnp.float32)
+        return top if exact else top.astype(jnp.bfloat16).astype(jnp.float32)
 
     def finish(i, top):
         parts, n = cuts(i)
@@ -118,7 +118,7 @@
         kept = jnp.where(at == 1, high, kept)
         stats[out, part : part + STEP] = jnp.where(at == 2, total - high, kept)
 
-    soft_step(scale, flags, qs, ks, vs, held, 0, emit)
+    soft_step(scale, flags, qs, ks, vs, held, 0, emit, False)
 
     @pl.when(head == heads - 1)
     def _():
@@ -165,7 +165,7 @@
         first = part // 64
         out[first : first + STEP // 64, hb] = value.astype(jnp.bfloat16).reshape(STEP // 64, 64, HD)
 
-    soft_step(scale, flags, qs, ks, vs, held, ROWS, emit)
+    soft_step(scale, flags, qs, ks, vs, held, ROWS, emit, True)
 
 
 def call(kernel, name, flags, first, last, wholes, pairs5, sides5, more, more_specs, out_shape, out_specs, keys, rows, scratch, share, aliases):
@@ -263,12 +263,8 @@
         own_sides.append(swap(pairs[i]))
     halos = [(lax.ppermute(p, "ta", t_up), lax.ppermute(p, "ta", t_down)) for p in pairs]
 
-    count = lax.axis_size(ALL_AXES)
-    text = jnp.concatenate([text_keys, text_values], 1)
-    text = jnp.broadcast_to(text[None], (count,) + text.shape)
-    text = lax.all_to_all(text, ALL_AXES, 0, 0, tiled=False).reshape(-1, 2 * chans)
-
-    halos[0], text = lax.optimization_barrier((halos[0], text))
+    text_pair = jnp.concatenate([text_keys, text_values], 1)
+    text_pair = jnp.broadcast_to(text_pair[None], (lax.axis_size(ALL_AXES),) + text_pair.shape)
     returned, sides = [], []
     for i, ((first, last), pair) in enumerate(zip(CHUNKS, pairs)):
         halo = halos[i]
@@ -276,7 +272,10 @@
             halo, _ = halos[i], _ = lax.optimization_barrier((halo, (ol, orr)))
         sides.append((own_sides[i], swap(halo[0]), swap(halo[1])))
         ol, orr = guests(flags, q_left, q_right, k, v, halo, sides[-1], first, last)
+        if i == 0:
+            ol, orr, text_pair = lax.optimization_barrier((ol, orr, text_pair))
         returned.append((lax.ppermute(orr, "wa", w_up), lax.ppermute(ol, "wa", w_down)))
+    text = lax.all_to_all(text_pair, ALL_AXES, 0, 0, tiled=False).reshape(-1, 2 * chans)
     out = None
     for (first, last), halo, side, (o_left, o_right) in zip(CHUNKS, halos, sides, returned):
         out = owns(flags, q, k, v, halo, side, text, o_left, o_right, out, first, last)

time: 134 us -> 130 us (0.970)
  the two profiles are of different devices: /device:TPU:62 before, /device:TPU:32 now
where the time goes in v3:
time: 130 us; the launch traced here: 129 us
  starting transfers between devices  46.9 us (36%)
  Pallas kernels  43.3 us (33%)
  waiting for transfers between devices  31.6 us (24%)
  local copies, waits for them, and re-layouts  7.07 us (5%)
    pallas_call x4, Pallas kernels, call(): pl.pallas_call(functools.partial(kernel, HD ** (-0.5) * LOG2E), grid_spec...  43.3 us
    ppermute x1, waiting for transfers between devices, per_device(): q_left = lax.ppermute(q, 'wa', w_up)  13.5 us
    all_to_all x1, starting transfers between devices, per_device(): lax.all_to_all(text_pair, ALL_AXES, 0, 0, tiled=False)  12.4 us
    ppermute x2, waiting for transfers between devices, per_device(): lax.ppermute(p, 'ta', t_down)  11.6 us
    ppermute x2, starting transfers between devices, per_device(): lax.ppermute(ol, 'wa', w_down)  10.8 us
    ppermute x2, starting transfers between devices, per_device(): lax.ppermute(p, 'ta', t_up)  7.17 us
    ppermute x2, waiting for transfers between devices, per_device(): lax.ppermute(p, 'ta', t_up)  6.54 us
    ppermute x2, starting transfers between devices, per_device(): lax.ppermute(orr, 'wa', w_up)  5.3 us
  transfers between devices with their start and end apart: 17, of which 4 were waited for; matrix products, arithmetic and copies ran while one was open for 2% of the time, Pallas kernels for 26%

profile of v3, /device:TPU:32, one launch (start us, length us, event | category | flops | bytes accessed | tf_op | source)
XLA Modules:
  0.0 129.3 jit_solution(12781440591593091556)
XLA Ops:
  0.0 1.5 %slice_bitcast_fusion = (bf16[1,4,2,64,384]{4,3,2,1,0:T(8,128)(2,1)S(1)}, bf16[1,4,2,64,384]{4,3,2,1,0:T(8,128)(2,1)S(1)}, bf16[1,4,2,64,384]{4,3,2,1,0:T(8,128)(2,1)S(1)}, bf16[1,4,2,64,384]{4,3,2,1,0:T(8,128)(2,1)S(1)}) fusion(bf16[4,2,64,768]{3,2,1,0:T(8,128)(2,1)} %bitcast.22, bf16[4,2,64,768]{3,2,1,0:T(8,128)(2,1)} %bitcast.17), kind=kLoop, calls=%fused_computation.2 | loop fusion | bytes 3145728 | tf_op jit(solution)/shard_map/stack | solution.py:259
  1.7 4.5 %collective-permute-start.5 = (bf16[2,4,2,64,384]{4,3,2,1,0:T(8,128)(2,1)S(1)}, bf16[2,4,2,64,384]{4,3,2,1,0:T(8,128)(2,1)}, u32[]{:S(2)}, u32[]{:S(2)}) collective-permute-start(bf16[2,4,2,64,384]{4,3,2,1,0:T(8,128)(2,1)S(1)} %pad_maximum_fusion), channel_id=1, source_target_pairs={{0,16},{16,32},{32,48},{48,64},{64,80},{80,96},{96,112},{1,17},{17... | collective-permute-start | bytes 2359304 | tf_op jit(solution)/shard_map/ppermute | solution.py:264
  6.2 1.3 collective-permute-start.6
  7.6 3.4 %collective-permute-start.3 = (bf16[4,2,64,768]{3,2,1,0:T(8,128)(2,1)S(1)}, bf16[4,2,64,768]{3,2,1,0:T(8,128)(2,1)}, u32[]{:S(2)}, u32[]{:S(2)}) collective-permute-start(bf16[4,2,64,768]{3,2,1,0:T(8,128)(2,1)S(1)} %bitcast.29), channel_id=1, source_target_pairs={{0,1},{1,2},{2,3},{3,4},{4,5},{5,6},{6,7},{8,9},{9,10},{10,11},{11... | collective-permute-start | bytes 2359304 | tf_op jit(solution)/shard_map/ppermute | solution.py:257
  11.0 4.6 %collective-permute-start.4 = (bf16[4,2,64,768]{3,2,1,0:T(8,128)(2,1)S(1)}, bf16[4,2,64,768]{3,2,1,0:T(8,128)(2,1)}, u32[]{:S(2)}, u32[]{:S(2)}) collective-permute-start(bf16[4,2,64,768]{3,2,1,0:T(8,128)(2,1)S(1)} %bitcast.30), channel_id=1, source_target_pairs={{1,0},{2,1},{3,2},{4,3},{5,4},{6,5},{7,6},{9,8},{10,9},{11,10},{12... | collective-permute-start | bytes 2359304 | tf_op jit(solution)/shard_map/ppermute | solution.py:258
  15.5 6.5 %collective-permute-done.5.minus = bf16[2,4,2,64,384]{4,3,2,1,0:T(8,128)(2,1)} collective-permute-done((bf16[2,4,2,64,384]{4,3,2,1,0:T(8,128)(2,1)S(1)}, bf16[2,4,2,64,384]{4,3,2,1,0:T(8,128)(2,1)}, u32[]{:S(2)}, u32[]{:S(2)}) %collective-permute-start.5) | collective-permute-done | bytes 786464 | tf_op jit(solution)/shard_map/ppermute | solution.py:264
  22.1 5.1 %collective-permute-done.6.plus = bf16[2,4,2,64,384]{4,3,2,1,0:T(8,128)(2,1)} collective-permute-done((bf16[2,4,2,64,384]{4,3,2,1,0:T(8,128)(2,1)S(1)}, bf16[2,4,2,64,384]{4,3,2,1,0:T(8,128)(2,1)}, u32[]{:S(2)}, u32[]{:S(2)}) %collective-permute-start.6) | collective-permute-done | bytes 786464 | tf_op jit(solution)/shard_map/ppermute | solution.py:264
  27.9 2.7 %collective-permute-start.1 = (bf16[2,4,2,64,384]{4,3,2,1,0:T(8,128)(2,1)S(1)}, bf16[2,4,2,64,384]{4,3,2,1,0:T(8,128)(2,1)S(1)}, u32[]{:S(2)}, u32[]{:S(2)}) collective-permute-start(bf16[2,4,2,64,384]{4,3,2,1,0:T(8,128)(2,1)S(1)} %pad_maximum_fusion.1), channel_id=1, source_target_pairs={{0,16},{16,32},{32,48},{48,64},{64,80},{80,96},{96,112},{1,17},{17... | collective-permute-start | bytes 2359304 | tf_op jit(solution)/shard_map/ppermute | solution.py:264
  30.5 13.5 %collective-permute-done.3.ql = bf16[4,2,64,768]{3,2,1,0:T(8,128)(2,1)} collective-permute-done((bf16[4,2,64,768]{3,2,1,0:T(8,128)(2,1)S(1)}, bf16[4,2,64,768]{3,2,1,0:T(8,128)(2,1)}, u32[]{:S(2)}, u32[]{:S(2)}) %collective-permute-start.3) | collective-permute-done | bytes 786464 | tf_op jit(solution)/shard_map/ppermute | solution.py:257
  44.0 1.3 collective-permute-start.2
  45.4 11.8 %guests_0.1 = (bf16[1632,128]{1,0:T(8,128)(2,1)}, bf16[1632,128]{1,0:T(8,128)(2,1)}) custom-call(s32[5]{0:T(128)} %stack.57.flags, bf16[4,2,64,768]{3,2,1,0:T(8,128)(2,1)} %collective-permute-done.3.ql, bf16[4,2,64,768]{3,2,1,0:T(8,128)(2,1)} %collective-permute-done.4.qr, bf16[4,2,64,768]{3,2,1,0:T(8,128)(2,1)} %bitcast.18, ...), custom_call_target="tpu_custom_call" | custom-call | flops 6039797760 | bytes 6000000 | tf_op jit(solution)/shard_map/guests_0/pallas_call | solution.py:177
  57.3 1.3 broadcast_in_dim.2
  58.6 6.5 %collective-permute-done.2.plus = bf16[2,4,2,64,384]{4,3,2,1,0:T(8,128)(2,1)} collective-permute-done((bf16[2,4,2,64,384]{4,3,2,1,0:T(8,128)(2,1)S(1)}, bf16[2,4,2,64,384]{4,3,2,1,0:T(8,128)(2,1)}, u32[]{:S(2)}, u32[]{:S(2)}) %collective-permute-start.2) | collective-permute-done | bytes 786464 | tf_op jit(solution)/shard_map/ppermute | solution.py:264
  65.6 12.4 %all-to-all-start = ((bf16[128,2,1536]{2,1,0:T(2,128)(2,1)}), bf16[128,2,1536]{2,1,0:T(2,128)(2,1)S(1)}, u32[]{:S(2)}, u32[]{:S(2)}) async-start(bf16[128,2,1536]{2,1,0:T(2,128)(2,1)} %broadcast_in_dim.2), calls=%async_computation | async-start | bytes 1572864 | tf_op jit(solution)/shard_map/all_to_all | solution.py:278
  78.0 3.4 %collective-permute-start.14 = (bf16[1632,128]{1,0:T(8,128)(2,1)}, bf16[1632,128]{1,0:T(8,128)(2,1)}, u32[]{:S(2)}, u32[]{:S(2)}) collective-permute-start(bf16[1632,128]{1,0:T(8,128)(2,1)} %get-tuple-element.21), channel_id=1, source_target_pairs={{0,1},{1,2},{2,3},{3,4},{4,5},{5,6},{6,7},{8,9},{9,10},{10,11},{11... | collective-permute-start | bytes 1253384 | tf_op jit(solution)/shard_map/ppermute | solution.py:277
  81.4 4.6 %collective-permute-start.15 = (bf16[1632,128]{1,0:T(8,128)(2,1)}, bf16[1632,128]{1,0:T(8,128)(2,1)}, u32[]{:S(2)}, u32[]{:S(2)}) collective-permute-start(bf16[1632,128]{1,0:T(8,128)(2,1)} %get-tuple-element.20), channel_id=1, source_target_pairs={{1,0},{2,1},{3,2},{4,3},{5,4},{6,5},{7,6},{9,8},{10,9},{11,10},{12... | collective-permute-start | bytes 1253384 | tf_op jit(solution)/shard_map/ppermute | solution.py:277
  86.0 0.9 copy-done.4
  86.9 11.8 %guests_3.1 = (bf16[1632,128]{1,0:T(8,128)(2,1)}, bf16[1632,128]{1,0:T(8,128)(2,1)}) custom-call(s32[5]{0:T(128)} %stack.57.flags, bf16[4,2,64,768]{3,2,1,0:T(8,128)(2,1)} %collective-permute-done.3.ql, bf16[4,2,64,768]{3,2,1,0:T(8,128)(2,1)} %collective-permute-done.4.qr, bf16[4,2,64,768]{3,2,1,0:T(8,128)(2,1)} %bitcast.19, ...), custom_call_target="tpu_custom_call" | custom-call | flops 6039797760 | bytes 6000000 | tf_op jit(solution)/shard_map/guests_3/pallas_call | solution.py:177
  98.7 1.9 %collective-permute-start.12 = (bf16[1632,128]{1,0:T(8,128)(2,1)}, bf16[1632,128]{1,0:T(8,128)(2,1)S(1)}, u32[]{:S(2)}, u32[]{:S(2)}) collective-permute-start(bf16[1632,128]{1,0:T(8,128)(2,1)} %get-tuple-element.25), channel_id=1, source_target_pairs={{0,1},{1,2},{2,3},{3,4},{4,5},{5,6},{6,7},{8,9},{9,10},{10,11},{11... | collective-permute-start | bytes 1253384 | tf_op jit(solution)/shard_map/ppermute | solution.py:277
  100.6 6.2 %collective-permute-start.13 = (bf16[1632,128]{1,0:T(8,128)(2,1)}, bf16[1632,128]{1,0:T(8,128)(2,1)S(1)}, u32[]{:S(2)}, u32[]{:S(2)}) collective-permute-start(bf16[1632,128]{1,0:T(8,128)(2,1)} %get-tuple-element.26), channel_id=1, source_target_pairs={{1,0},{2,1},{3,2},{4,3},{5,4},{6,5},{7,6},{9,8},{10,9},{11,10},{12... | collective-permute-start | bytes 1253384 | tf_op jit(solution)/shard_map/ppermute | solution.py:277
  106.9 1.2 reshape.19.tk.tv
  108.1 9.8 %owns_0.1.rest_0_ = bf16[4,2,64,768]{3,2,1,0:T(8,128)(2,1)} custom-call(s32[5]{0:T(128)} %stack.57.flags, bf16[4,2,64,768]{3,2,1,0:T(8,128)(2,1)} %bitcast.27, bf16[4,2,64,768]{3,2,1,0:T(8,128)(2,1)} %bitcast.20, bf16[4,2,64,768]{3,2,1,0:T(8,128)(2,1)} %bitcast.25, bf16[2,4,2,64,384]{4,3,2,1,0:T(8,128)(2,1)} %collective-permute-done.5.minus, ...), custom_call_target="tpu_custom_call" | custom-call | flops 3422552064 | bytes 6000000 | tf_op jit(solution)/shard_map/owns_0/pallas_call | solution.py:177
  118.7 0.8 copy-done.6
  119.5 9.8 %owns_3.1 = bf16[4,2,64,768]{3,2,1,0:T(8,128)(2,1)} custom-call(s32[5]{0:T(128)} %stack.57.flags, bf16[4,2,64,768]{3,2,1,0:T(8,128)(2,1)} %bitcast.28, bf16[4,2,64,768]{3,2,1,0:T(8,128)(2,1)} %bitcast.21, bf16[4,2,64,768]{3,2,1,0:T(8,128)(2,1)} %bitcast.26, bf16[2,4,2,64,384]{4,3,2,1,0:T(8,128)(2,1)} %copy-done.3, ...), custom_call_target="tpu_custom_call", output_to_operand_aliasing={{}: (13, {})} | custom-call | flops 3422552064 | bytes 6000000 | tf_op jit(solution)/shard_map/owns_3/pallas_call | solution.py:177
  (35 shorter events, 2.3 us)
Async XLA Ops:
  1.6 6.0 %copy-start.2 = (bf16[4,16,8,768]{3,2,1,0:T(8,128)(2,1)S(1)}, bf16[4,16,8,768]{3,2,1,0:T(8,128)(2,1)}, u32[]{:S(2)}) copy-start(bf16[4,16,8,768]{3,2,1,0:T(8,128)(2,1)} %param.5) | copy-start | bytes 2359300
  1.7 20.4 %collective-permute-start.5 = (bf16[2,4,2,64,384]{4,3,2,1,0:T(8,128)(2,1)S(1)}, bf16[2,4,2,64,384]{4,3,2,1,0:T(8,128)(2,1)}, u32[]{:S(2)}, u32[]{:S(2)}) collective-permute-start(bf16[2,4,2,64,384]{4,3,2,1,0:T(8,128)(2,1)S(1)} %pad_maximum_fusion), channel_id=1, source_target_pairs={{0,16},{16,32},{32,48},{48,64},{64,80},{80,96},{96,112},{1,17},{17... | collective-permute-start | bytes 2359304 | tf_op jit(solution)/shard_map/ppermute | solution.py:264
  6.2 21.0 %collective-permute-start.6 = (bf16[2,4,2,64,384]{4,3,2,1,0:T(8,128)(2,1)S(1)}, bf16[2,4,2,64,384]{4,3,2,1,0:T(8,128)(2,1)}, u32[]{:S(2)}, u32[]{:S(2)}) collective-permute-start(bf16[2,4,2,64,384]{4,3,2,1,0:T(8,128)(2,1)S(1)} %pad_maximum_fusion), channel_id=1, source_target_pairs={{16,0},{32,16},{48,32},{64,48},{80,64},{96,80},{112,96},{17,1},{33... | collective-permute-start | bytes 2359304 | tf_op jit(solution)/shard_map/ppermute | solution.py:264
  7.5 20.4 %collective-permute-start = (bf16[2,4,2,64,384]{4,3,2,1,0:T(8,128)(2,1)S(1)}, bf16[2,4,2,64,384]{4,3,2,1,0:T(8,128)(2,1)}, u32[]{:S(2)}, u32[]{:S(2)}) collective-permute-start(bf16[2,4,2,64,384]{4,3,2,1,0:T(8,128)(2,1)S(1)} %pad_maximum_fusion), channel_id=1, source_target_pairs={{0,8},{8,0},{1,9},{9,1},{2,10},{10,2},{3,11},{11,3},{4,12},{12,4},... | collective-permute-start | bytes 2359304 | tf_op jit(solution)/shard_map/ppermute | solution.py:255
  7.6 36.4 %collective-permute-start.3 = (bf16[4,2,64,768]{3,2,1,0:T(8,128)(2,1)S(1)}, bf16[4,2,64,768]{3,2,1,0:T(8,128)(2,1)}, u32[]{:S(2)}, u32[]{:S(2)}) collective-permute-start(bf16[4,2,64,768]{3,2,1,0:T(8,128)(2,1)S(1)} %bitcast.29), channel_id=1, source_target_pairs={{0,1},{1,2},{2,3},{3,4},{4,5},{5,6},{6,7},{8,9},{9,10},{10,11},{11... | collective-permute-start | bytes 2359304 | tf_op jit(solution)/shard_map/ppermute | solution.py:257
  11.0 34.4 %collective-permute-start.4 = (bf16[4,2,64,768]{3,2,1,0:T(8,128)(2,1)S(1)}, bf16[4,2,64,768]{3,2,1,0:T(8,128)(2,1)}, u32[]{:S(2)}, u32[]{:S(2)}) collective-permute-start(bf16[4,2,64,768]{3,2,1,0:T(8,128)(2,1)S(1)} %bitcast.30), channel_id=1, source_target_pairs={{1,0},{2,1},{3,2},{4,3},{5,4},{6,5},{7,6},{9,8},{10,9},{11,10},{12... | collective-permute-start | bytes 2359304 | tf_op jit(solution)/shard_map/ppermute | solution.py:258
  22.1 23.4 %collective-permute-start.7 = (bf16[2,4,2,64,384]{4,3,2,1,0:T(8,128)(2,1)}, bf16[2,4,2,64,384]{4,3,2,1,0:T(8,128)(2,1)}, u32[]{:S(2)}, u32[]{:S(2)}) collective-permute-start(bf16[2,4,2,64,384]{4,3,2,1,0:T(8,128)(2,1)} %collective-permute-done.5.minus), channel_id=1, source_target_pairs={{0,8},{8,0},{1,9},{9,1},{2,10},{10,2},{3,11},{11,3},{4,12},{12,4},... | collective-permute-start | bytes 2359304 | tf_op jit(solution)/shard_map/ppermute | solution.py:255
  27.2 18.3 %collective-permute-start.8 = (bf16[2,4,2,64,384]{4,3,2,1,0:T(8,128)(2,1)}, bf16[2,4,2,64,384]{4,3,2,1,0:T(8,128)(2,1)}, u32[]{:S(2)}, u32[]{:S(2)}) collective-permute-start(bf16[2,4,2,64,384]{4,3,2,1,0:T(8,128)(2,1)} %collective-permute-done.6.plus), channel_id=1, source_target_pairs={{0,8},{8,0},{1,9},{9,1},{2,10},{10,2},{3,11},{11,3},{4,12},{12,4},... | collective-permute-start | bytes 2359304 | tf_op jit(solution)/shard_map/ppermute | solution.py:255
  27.8 17.5 %copy-start = (bf16[2,768]{1,0:T(2,128)(2,1)S(1)}, bf16[2,768]{1,0:T(2,128)(2,1)}, u32[]{:S(2)}) copy-start(bf16[2,768]{1,0:T(2,128)(2,1)} %param.9) | copy-start | bytes 9220
  27.8 17.5 %copy-start.1 = (bf16[2,768]{1,0:T(2,128)(2,1)S(1)}, bf16[2,768]{1,0:T(2,128)(2,1)}, u32[]{:S(2)}) copy-start(bf16[2,768]{1,0:T(2,128)(2,1)} %param.8) | copy-start | bytes 9220
  27.9 30.7 %collective-permute-start.1 = (bf16[2,4,2,64,384]{4,3,2,1,0:T(8,128)(2,1)S(1)}, bf16[2,4,2,64,384]{4,3,2,1,0:T(8,128)(2,1)S(1)}, u32[]{:S(2)}, u32[]{:S(2)}) collective-permute-start(bf16[2,4,2,64,384]{4,3,2,1,0:T(8,128)(2,1)S(1)} %pad_maximum_fusion.1), channel_id=1, source_target_pairs={{0,16},{16,32},{32,48},{48,64},{64,80},{80,96},{96,112},{1,17},{17... | collective-permute-start | bytes 2359304 | tf_op jit(solution)/shard_map/ppermute | solution.py:264
  44.0 21.1 %collective-permute-start.2 = (bf16[2,4,2,64,384]{4,3,2,1,0:T(8,128)(2,1)S(1)}, bf16[2,4,2,64,384]{4,3,2,1,0:T(8,128)(2,1)}, u32[]{:S(2)}, u32[]{:S(2)}) collective-permute-start(bf16[2,4,2,64,384]{4,3,2,1,0:T(8,128)(2,1)S(1)} %pad_maximum_fusion.1), channel_id=1, source_target_pairs={{16,0},{32,16},{48,32},{64,48},{80,64},{96,80},{112,96},{17,1},{33... | collective-permute-start | bytes 2359304 | tf_op jit(solution)/shard_map/ppermute | solution.py:264
  45.3 40.7 %collective-permute-start.9 = (bf16[2,4,2,64,384]{4,3,2,1,0:T(8,128)(2,1)S(1)}, bf16[2,4,2,64,384]{4,3,2,1,0:T(8,128)(2,1)S(1)}, u32[]{:S(2)}, u32[]{:S(2)}) collective-permute-start(bf16[2,4,2,64,384]{4,3,2,1,0:T(8,128)(2,1)S(1)} %pad_maximum_fusion.1), channel_id=1, source_target_pairs={{0,8},{8,0},{1,9},{9,1},{2,10},{10,2},{3,11},{11,3},{4,12},{12,4},... | collective-permute-start | bytes 2359304 | tf_op jit(solution)/shard_map/ppermute | solution.py:255
  58.6 7.0 %copy-start.3 = (bf16[2,4,2,64,384]{4,3,2,1,0:T(8,128)(2,1)}, bf16[2,4,2,64,384]{4,3,2,1,0:T(8,128)(2,1)S(1)}, u32[]{:S(2)}) copy-start(bf16[2,4,2,64,384]{4,3,2,1,0:T(8,128)(2,1)S(1)} %collective-permute-done.1.minus) | copy-start | bytes 2359300
  65.1 20.9 %collective-permute-start.10 = (bf16[2,4,2,64,384]{4,3,2,1,0:T(8,128)(2,1)S(1)}, bf16[2,4,2,64,384]{4,3,2,1,0:T(8,128)(2,1)}, u32[]{:S(2)}, u32[]{:S(2)}) collective-permute-start(bf16[2,4,2,64,384]{4,3,2,1,0:T(8,128)(2,1)S(1)} %collective-permute-done.1.minus), channel_id=1, source_target_pairs={{0,8},{8,0},{1,9},{9,1},{2,10},{10,2},{3,11},{11,3},{4,12},{12,4},... | collective-permute-start | bytes 2359304 | tf_op jit(solution)/shard_map/ppermute | solution.py:255
  65.1 20.9 %collective-permute-start.11 = (bf16[2,4,2,64,384]{4,3,2,1,0:T(8,128)(2,1)}, bf16[2,4,2,64,384]{4,3,2,1,0:T(8,128)(2,1)}, u32[]{:S(2)}, u32[]{:S(2)}) collective-permute-start(bf16[2,4,2,64,384]{4,3,2,1,0:T(8,128)(2,1)} %collective-permute-done.2.plus), channel_id=1, source_target_pairs={{0,8},{8,0},{1,9},{9,1},{2,10},{10,2},{3,11},{11,3},{4,12},{12,4},... | collective-permute-start | bytes 2359304 | tf_op jit(solution)/shard_map/ppermute | solution.py:255
  65.6 41.3 %all-to-all-start = ((bf16[128,2,1536]{2,1,0:T(2,128)(2,1)}), bf16[128,2,1536]{2,1,0:T(2,128)(2,1)S(1)}, u32[]{:S(2)}, u32[]{:S(2)}) async-start(bf16[128,2,1536]{2,1,0:T(2,128)(2,1)} %broadcast_in_dim.2), calls=%async_computation | async-start | bytes 1572864 | tf_op jit(solution)/shard_map/all_to_all | solution.py:278
  78.0 30.1 %collective-permute-start.14 = (bf16[1632,128]{1,0:T(8,128)(2,1)}, bf16[1632,128]{1,0:T(8,128)(2,1)}, u32[]{:S(2)}, u32[]{:S(2)}) collective-permute-start(bf16[1632,128]{1,0:T(8,128)(2,1)} %get-tuple-element.21), channel_id=1, source_target_pairs={{0,1},{1,2},{2,3},{3,4},{4,5},{5,6},{6,7},{8,9},{9,10},{10,11},{11... | collective-permute-start | bytes 1253384 | tf_op jit(solution)/shard_map/ppermute | solution.py:277
  81.4 26.7 %collective-permute-start.15 = (bf16[1632,128]{1,0:T(8,128)(2,1)}, bf16[1632,128]{1,0:T(8,128)(2,1)}, u32[]{:S(2)}, u32[]{:S(2)}) collective-permute-start(bf16[1632,128]{1,0:T(8,128)(2,1)} %get-tuple-element.20), channel_id=1, source_target_pairs={{1,0},{2,1},{3,2},{4,3},{5,4},{6,5},{7,6},{9,8},{10,9},{11,10},{12... | collective-permute-start | bytes 1253384 | tf_op jit(solution)/shard_map/ppermute | solution.py:277
  86.0 0.9 copy-start.4
  98.7 19.2 %collective-permute-start.12 = (bf16[1632,128]{1,0:T(8,128)(2,1)}, bf16[1632,128]{1,0:T(8,128)(2,1)S(1)}, u32[]{:S(2)}, u32[]{:S(2)}) collective-permute-start(bf16[1632,128]{1,0:T(8,128)(2,1)} %get-tuple-element.25), channel_id=1, source_target_pairs={{0,1},{1,2},{2,3},{3,4},{4,5},{5,6},{6,7},{8,9},{9,10},{10,11},{11... | collective-permute-start | bytes 1253384 | tf_op jit(solution)/shard_map/ppermute | solution.py:277
  100.6 17.3 %collective-permute-start.13 = (bf16[1632,128]{1,0:T(8,128)(2,1)}, bf16[1632,128]{1,0:T(8,128)(2,1)S(1)}, u32[]{:S(2)}, u32[]{:S(2)}) collective-permute-start(bf16[1632,128]{1,0:T(8,128)(2,1)} %get-tuple-element.26), channel_id=1, source_target_pairs={{1,0},{2,1},{3,2},{4,3},{5,4},{6,5},{7,6},{9,8},{10,9},{11,10},{12... | collective-permute-start | bytes 1253384 | tf_op jit(solution)/shard_map/ppermute | solution.py:277
  117.9 0.8 copy-start.5
  118.7 0.8 copy-start.6

commit v4 on v3

--- a/solution.py
+++ b/solution.py
@@ -42,7 +42,10 @@
         ks[at : at + rows] = kk.reshape(rows, HD)
         vs[at : at + rows, :HD] = vv.reshape(rows, HD)
         at += rows
-    vs[:, HD:] = jnp.ones((vs.shape[0], HD), jnp.bfloat16)
+
+    @pl.when(pl.program_id(0) == 0)
+    def _():
+        vs[:, HD:] = jnp.ones((vs.shape[0], HD), jnp.bfloat16)
 
 
 def soft_step(scale, flags, qs, ks, vs, held, text, emit, exact):

time: 130 us -> 130 us (level)
  transfers between devices with their start and end apart: 17 -> 17, of which waited for: 4 -> 4; matrix products, arithmetic and copies ran while one was open for 2% -> 3% of each run, Pallas kernels for 26% -> 26%
where the time goes in v4:
time: 130 us; the launch traced here: 129 us
  starting transfers between devices  46.9 us (36%)
  Pallas kernels  42.9 us (33%)
  waiting for transfers between devices  31.7 us (24%)
  local copies, waits for them, and re-layouts  7.07 us (5%)
    pallas_call x4, Pallas kernels, call(): pl.pallas_call(functools.partial(kernel, HD ** (-0.5) * LOG2E), grid_spec...  42.9 us
    ppermute x1, waiting for transfers between devices, per_device(): q_left = lax.ppermute(q, 'wa', w_up)  13.5 us
    all_to_all x1, starting transfers between devices, per_device(): lax.all_to_all(text_pair, ALL_AXES, 0, 0, tiled=False)  12.4 us
    ppermute x2, waiting for transfers between devices, per_device(): lax.ppermute(p, 'ta', t_down)  11.7 us
    ppermute x2, starting transfers between devices, per_device(): lax.ppermute(ol, 'wa', w_down)  10.8 us
    ppermute x2, starting transfers between devices, per_device(): lax.ppermute(p, 'ta', t_up)  7.17 us
    ppermute x2, waiting for transfers between devices, per_device(): lax.ppermute(p, 'ta', t_up)  6.54 us
    ppermute x2, starting transfers between devices, per_device(): lax.ppermute(orr, 'wa', w_up)  5.3 us
  transfers between devices with their start and end apart: 17, of which 4 were waited for; matrix products, arithmetic and copies ran while one was open for 3% of the time, Pallas kernels for 26%

profile of v4, /device:TPU:32, one launch (start us, length us, event | category | flops | bytes accessed | tf_op | source)
XLA Modules:
  0.0 129.0 jit_solution(11524686258108992436)
XLA Ops:
  0.0 1.5 %slice_bitcast_fusion = (bf16[1,4,2,64,384]{4,3,2,1,0:T(8,128)(2,1)S(1)}, bf16[1,4,2,64,384]{4,3,2,1,0:T(8,128)(2,1)S(1)}, bf16[1,4,2,64,384]{4,3,2,1,0:T(8,128)(2,1)S(1)}, bf16[1,4,2,64,384]{4,3,2,1,0:T(8,128)(2,1)S(1)}) fusion(bf16[4,2,64,768]{3,2,1,0:T(8,128)(2,1)} %bitcast.22, bf16[4,2,64,768]{3,2,1,0:T(8,128)(2,1)} %bitcast.17), kind=kLoop, calls=%fused_computation.2 | loop fusion | bytes 3145728 | tf_op jit(solution)/shard_map/stack | solution.py:262
  1.7 4.5 %collective-permute-start.5 = (bf16[2,4,2,64,384]{4,3,2,1,0:T(8,128)(2,1)S(1)}, bf16[2,4,2,64,384]{4,3,2,1,0:T(8,128)(2,1)}, u32[]{:S(2)}, u32[]{:S(2)}) collective-permute-start(bf16[2,4,2,64,384]{4,3,2,1,0:T(8,128)(2,1)S(1)} %pad_maximum_fusion), channel_id=1, source_target_pairs={{0,16},{16,32},{32,48},{48,64},{64,80},{80,96},{96,112},{1,17},{17... | collective-permute-start | bytes 2359304 | tf_op jit(solution)/shard_map/ppermute | solution.py:267
  6.2 1.3 collective-permute-start.6
  7.6 3.4 %collective-permute-start.3 = (bf16[4,2,64,768]{3,2,1,0:T(8,128)(2,1)S(1)}, bf16[4,2,64,768]{3,2,1,0:T(8,128)(2,1)}, u32[]{:S(2)}, u32[]{:S(2)}) collective-permute-start(bf16[4,2,64,768]{3,2,1,0:T(8,128)(2,1)S(1)} %bitcast.29), channel_id=1, source_target_pairs={{0,1},{1,2},{2,3},{3,4},{4,5},{5,6},{6,7},{8,9},{9,10},{10,11},{11... | collective-permute-start | bytes 2359304 | tf_op jit(solution)/shard_map/ppermute | solution.py:260
  11.0 4.6 %collective-permute-start.4 = (bf16[4,2,64,768]{3,2,1,0:T(8,128)(2,1)S(1)}, bf16[4,2,64,768]{3,2,1,0:T(8,128)(2,1)}, u32[]{:S(2)}, u32[]{:S(2)}) collective-permute-start(bf16[4,2,64,768]{3,2,1,0:T(8,128)(2,1)S(1)} %bitcast.30), channel_id=1, source_target_pairs={{1,0},{2,1},{3,2},{4,3},{5,4},{6,5},{7,6},{9,8},{10,9},{11,10},{12... | collective-permute-start | bytes 2359304 | tf_op jit(solution)/shard_map/ppermute | solution.py:261
  15.5 6.5 %collective-permute-done.5.minus = bf16[2,4,2,64,384]{4,3,2,1,0:T(8,128)(2,1)} collective-permute-done((bf16[2,4,2,64,384]{4,3,2,1,0:T(8,128)(2,1)S(1)}, bf16[2,4,2,64,384]{4,3,2,1,0:T(8,128)(2,1)}, u32[]{:S(2)}, u32[]{:S(2)}) %collective-permute-start.5) | collective-permute-done | bytes 786464 | tf_op jit(solution)/shard_map/ppermute | solution.py:267
  22.1 5.1 %collective-permute-done.6.plus = bf16[2,4,2,64,384]{4,3,2,1,0:T(8,128)(2,1)} collective-permute-done((bf16[2,4,2,64,384]{4,3,2,1,0:T(8,128)(2,1)S(1)}, bf16[2,4,2,64,384]{4,3,2,1,0:T(8,128)(2,1)}, u32[]{:S(2)}, u32[]{:S(2)}) %collective-permute-start.6) | collective-permute-done | bytes 786464 | tf_op jit(solution)/shard_map/ppermute | solution.py:267
  27.9 2.7 %collective-permute-start.1 = (bf16[2,4,2,64,384]{4,3,2,1,0:T(8,128)(2,1)S(1)}, bf16[2,4,2,64,384]{4,3,2,1,0:T(8,128)(2,1)S(1)}, u32[]{:S(2)}, u32[]{:S(2)}) collective-permute-start(bf16[2,4,2,64,384]{4,3,2,1,0:T(8,128)(2,1)S(1)} %pad_maximum_fusion.1), channel_id=1, source_target_pairs={{0,16},{16,32},{32,48},{48,64},{64,80},{80,96},{96,112},{1,17},{17... | collective-permute-start | bytes 2359304 | tf_op jit(solution)/shard_map/ppermute | solution.py:267
  30.5 13.5 %collective-permute-done.3.ql = bf16[4,2,64,768]{3,2,1,0:T(8,128)(2,1)} collective-permute-done((bf16[4,2,64,768]{3,2,1,0:T(8,128)(2,1)S(1)}, bf16[4,2,64,768]{3,2,1,0:T(8,128)(2,1)}, u32[]{:S(2)}, u32[]{:S(2)}) %collective-permute-start.3) | collective-permute-done | bytes 786464 | tf_op jit(solution)/shard_map/ppermute | solution.py:260
  44.0 1.3 collective-permute-start.2
  45.4 11.7 %guests_0.1 = (bf16[1632,128]{1,0:T(8,128)(2,1)}, bf16[1632,128]{1,0:T(8,128)(2,1)}) custom-call(s32[5]{0:T(128)} %stack.57.flags, bf16[4,2,64,768]{3,2,1,0:T(8,128)(2,1)} %collective-permute-done.3.ql, bf16[4,2,64,768]{3,2,1,0:T(8,128)(2,1)} %collective-permute-done.4.qr, bf16[4,2,64,768]{3,2,1,0:T(8,128)(2,1)} %bitcast.18, ...), custom_call_target="tpu_custom_call" | custom-call | flops 6039797760 | bytes 6000000 | tf_op jit(solution)/shard_map/guests_0/pallas_call | solution.py:180
  57.2 1.3 broadcast_in_dim.2
  58.5 6.6 %collective-permute-done.2.plus = bf16[2,4,2,64,384]{4,3,2,1,0:T(8,128)(2,1)} collective-permute-done((bf16[2,4,2,64,384]{4,3,2,1,0:T(8,128)(2,1)S(1)}, bf16[2,4,2,64,384]{4,3,2,1,0:T(8,128)(2,1)}, u32[]{:S(2)}, u32[]{:S(2)}) %collective-permute-start.2) | collective-permute-done | bytes 786464 | tf_op jit(solution)/shard_map/ppermute | solution.py:267
  65.6 12.4 %all-to-all-start = ((bf16[128,2,1536]{2,1,0:T(2,128)(2,1)}), bf16[128,2,1536]{2,1,0:T(2,128)(2,1)S(1)}, u32[]{:S(2)}, u32[]{:S(2)}) async-start(bf16[128,2,1536]{2,1,0:T(2,128)(2,1)} %broadcast_in_dim.2), calls=%async_computation | async-start | bytes 1572864 | tf_op jit(solution)/shard_map/all_to_all | solution.py:281
  78.0 3.4 %collective-permute-start.14 = (bf16[1632,128]{1,0:T(8,128)(2,1)}, bf16[1632,128]{1,0:T(8,128)(2,1)}, u32[]{:S(2)}, u32[]{:S(2)}) collective-permute-start(bf16[1632,128]{1,0:T(8,128)(2,1)} %get-tuple-element.21), channel_id=1, source_target_pairs={{0,1},{1,2},{2,3},{3,4},{4,5},{5,6},{6,7},{8,9},{9,10},{10,11},{11... | collective-permute-start | bytes 1253384 | tf_op jit(solution)/shard_map/ppermute | solution.py:280
  81.4 4.6 %collective-permute-start.15 = (bf16[1632,128]{1,0:T(8,128)(2,1)}, bf16[1632,128]{1,0:T(8,128)(2,1)}, u32[]{:S(2)}, u32[]{:S(2)}) collective-permute-start(bf16[1632,128]{1,0:T(8,128)(2,1)} %get-tuple-element.20), channel_id=1, source_target_pairs={{1,0},{2,1},{3,2},{4,3},{5,4},{6,5},{7,6},{9,8},{10,9},{11,10},{12... | collective-permute-start | bytes 1253384 | tf_op jit(solution)/shard_map/ppermute | solution.py:280
  86.0 0.9 copy-done.4
  86.9 11.7 %guests_3.1 = (bf16[1632,128]{1,0:T(8,128)(2,1)}, bf16[1632,128]{1,0:T(8,128)(2,1)}) custom-call(s32[5]{0:T(128)} %stack.57.flags, bf16[4,2,64,768]{3,2,1,0:T(8,128)(2,1)} %collective-permute-done.3.ql, bf16[4,2,64,768]{3,2,1,0:T(8,128)(2,1)} %collective-permute-done.4.qr, bf16[4,2,64,768]{3,2,1,0:T(8,128)(2,1)} %bitcast.19, ...), custom_call_target="tpu_custom_call" | custom-call | flops 6039797760 | bytes 6000000 | tf_op jit(solution)/shard_map/guests_3/pallas_call | solution.py:180
  98.6 1.9 %collective-permute-start.12 = (bf16[1632,128]{1,0:T(8,128)(2,1)}, bf16[1632,128]{1,0:T(8,128)(2,1)S(1)}, u32[]{:S(2)}, u32[]{:S(2)}) collective-permute-start(bf16[1632,128]{1,0:T(8,128)(2,1)} %get-tuple-element.25), channel_id=1, source_target_pairs={{0,1},{1,2},{2,3},{3,4},{4,5},{5,6},{6,7},{8,9},{9,10},{10,11},{11... | collective-permute-start | bytes 1253384 | tf_op jit(solution)/shard_map/ppermute | solution.py:280
  100.5 6.2 %collective-permute-start.13 = (bf16[1632,128]{1,0:T(8,128)(2,1)}, bf16[1632,128]{1,0:T(8,128)(2,1)S(1)}, u32[]{:S(2)}, u32[]{:S(2)}) collective-permute-start(bf16[1632,128]{1,0:T(8,128)(2,1)} %get-tuple-element.26), channel_id=1, source_target_pairs={{1,0},{2,1},{3,2},{4,3},{5,4},{6,5},{7,6},{9,8},{10,9},{11,10},{12... | collective-permute-start | bytes 1253384 | tf_op jit(solution)/shard_map/ppermute | solution.py:280
  106.8 1.2 reshape.19.tk.tv
  108.0 9.7 %owns_0.1.rest_0_ = bf16[4,2,64,768]{3,2,1,0:T(8,128)(2,1)} custom-call(s32[5]{0:T(128)} %stack.57.flags, bf16[4,2,64,768]{3,2,1,0:T(8,128)(2,1)} %bitcast.27, bf16[4,2,64,768]{3,2,1,0:T(8,128)(2,1)} %bitcast.20, bf16[4,2,64,768]{3,2,1,0:T(8,128)(2,1)} %bitcast.25, bf16[2,4,2,64,384]{4,3,2,1,0:T(8,128)(2,1)} %collective-permute-done.5.minus, ...), custom_call_target="tpu_custom_call" | custom-call | flops 3422552064 | bytes 6000000 | tf_op jit(solution)/shard_map/owns_0/pallas_call | solution.py:180
  118.5 0.8 copy-done.6
  119.3 9.7 %owns_3.1 = bf16[4,2,64,768]{3,2,1,0:T(8,128)(2,1)} custom-call(s32[5]{0:T(128)} %stack.57.flags, bf16[4,2,64,768]{3,2,1,0:T(8,128)(2,1)} %bitcast.28, bf16[4,2,64,768]{3,2,1,0:T(8,128)(2,1)} %bitcast.21, bf16[4,2,64,768]{3,2,1,0:T(8,128)(2,1)} %bitcast.26, bf16[2,4,2,64,384]{4,3,2,1,0:T(8,128)(2,1)} %copy-done.3, ...), custom_call_target="tpu_custom_call", output_to_operand_aliasing={{}: (13, {})} | custom-call | flops 3422552064 | bytes 6000000 | tf_op jit(solution)/shard_map/owns_3/pallas_call | solution.py:180
  (35 shorter events, 2.3 us)
Async XLA Ops:
  1.6 6.0 %copy-start.2 = (bf16[4,16,8,768]{3,2,1,0:T(8,128)(2,1)S(1)}, bf16[4,16,8,768]{3,2,1,0:T(8,128)(2,1)}, u32[]{:S(2)}) copy-start(bf16[4,16,8,768]{3,2,1,0:T(8,128)(2,1)} %param.5) | copy-start | bytes 2359300
  1.7 20.4 %collective-permute-start.5 = (bf16[2,4,2,64,384]{4,3,2,1,0:T(8,128)(2,1)S(1)}, bf16[2,4,2,64,384]{4,3,2,1,0:T(8,128)(2,1)}, u32[]{:S(2)}, u32[]{:S(2)}) collective-permute-start(bf16[2,4,2,64,384]{4,3,2,1,0:T(8,128)(2,1)S(1)} %pad_maximum_fusion), channel_id=1, source_target_pairs={{0,16},{16,32},{32,48},{48,64},{64,80},{80,96},{96,112},{1,17},{17... | collective-permute-start | bytes 2359304 | tf_op jit(solution)/shard_map/ppermute | solution.py:267
  6.2 21.0 %collective-permute-start.6 = (bf16[2,4,2,64,384]{4,3,2,1,0:T(8,128)(2,1)S(1)}, bf16[2,4,2,64,384]{4,3,2,1,0:T(8,128)(2,1)}, u32[]{:S(2)}, u32[]{:S(2)}) collective-permute-start(bf16[2,4,2,64,384]{4,3,2,1,0:T(8,128)(2,1)S(1)} %pad_maximum_fusion), channel_id=1, source_target_pairs={{16,0},{32,16},{48,32},{64,48},{80,64},{96,80},{112,96},{17,1},{33... | collective-permute-start | bytes 2359304 | tf_op jit(solution)/shard_map/ppermute | solution.py:267
  7.5 20.4 %collective-permute-start = (bf16[2,4,2,64,384]{4,3,2,1,0:T(8,128)(2,1)S(1)}, bf16[2,4,2,64,384]{4,3,2,1,0:T(8,128)(2,1)}, u32[]{:S(2)}, u32[]{:S(2)}) collective-permute-start(bf16[2,4,2,64,384]{4,3,2,1,0:T(8,128)(2,1)S(1)} %pad_maximum_fusion), channel_id=1, source_target_pairs={{0,8},{8,0},{1,9},{9,1},{2,10},{10,2},{3,11},{11,3},{4,12},{12,4},... | collective-permute-start | bytes 2359304 | tf_op jit(solution)/shard_map/ppermute | solution.py:258
  7.6 36.4 %collective-permute-start.3 = (bf16[4,2,64,768]{3,2,1,0:T(8,128)(2,1)S(1)}, bf16[4,2,64,768]{3,2,1,0:T(8,128)(2,1)}, u32[]{:S(2)}, u32[]{:S(2)}) collective-permute-start(bf16[4,2,64,768]{3,2,1,0:T(8,128)(2,1)S(1)} %bitcast.29), channel_id=1, source_target_pairs={{0,1},{1,2},{2,3},{3,4},{4,5},{5,6},{6,7},{8,9},{9,10},{10,11},{11... | collective-permute-start | bytes 2359304 | tf_op jit(solution)/shard_map/ppermute | solution.py:260
  11.0 34.4 %collective-permute-start.4 = (bf16[4,2,64,768]{3,2,1,0:T(8,128)(2,1)S(1)}, bf16[4,2,64,768]{3,2,1,0:T(8,128)(2,1)}, u32[]{:S(2)}, u32[]{:S(2)}) collective-permute-start(bf16[4,2,64,768]{3,2,1,0:T(8,128)(2,1)S(1)} %bitcast.30), channel_id=1, source_target_pairs={{1,0},{2,1},{3,2},{4,3},{5,4},{6,5},{7,6},{9,8},{10,9},{11,10},{12... | collective-permute-start | bytes 2359304 | tf_op jit(solution)/shard_map/ppermute | solution.py:261
  22.1 23.4 %collective-permute-start.7 = (bf16[2,4,2,64,384]{4,3,2,1,0:T(8,128)(2,1)}, bf16[2,4,2,64,384]{4,3,2,1,0:T(8,128)(2,1)}, u32[]{:S(2)}, u32[]{:S(2)}) collective-permute-start(bf16[2,4,2,64,384]{4,3,2,1,0:T(8,128)(2,1)} %collective-permute-done.5.minus), channel_id=1, source_target_pairs={{0,8},{8,0},{1,9},{9,1},{2,10},{10,2},{3,11},{11,3},{4,12},{12,4},... | collective-permute-start | bytes 2359304 | tf_op jit(solution)/shard_map/ppermute | solution.py:258
  27.2 18.3 %collective-permute-start.8 = (bf16[2,4,2,64,384]{4,3,2,1,0:T(8,128)(2,1)}, bf16[2,4,2,64,384]{4,3,2,1,0:T(8,128)(2,1)}, u32[]{:S(2)}, u32[]{:S(2)}) collective-permute-start(bf16[2,4,2,64,384]{4,3,2,1,0:T(8,128)(2,1)} %collective-permute-done.6.plus), channel_id=1, source_target_pairs={{0,8},{8,0},{1,9},{9,1},{2,10},{10,2},{3,11},{11,3},{4,12},{12,4},... | collective-permute-start | bytes 2359304 | tf_op jit(solution)/shard_map/ppermute | solution.py:258
  27.8 17.5 %copy-start = (bf16[2,768]{1,0:T(2,128)(2,1)S(1)}, bf16[2,768]{1,0:T(2,128)(2,1)}, u32[]{:S(2)}) copy-start(bf16[2,768]{1,0:T(2,128)(2,1)} %param.9) | copy-start | bytes 9220
  27.8 17.5 %copy-start.1 = (bf16[2,768]{1,0:T(2,128)(2,1)S(1)}, bf16[2,768]{1,0:T(2,128)(2,1)}, u32[]{:S(2)}) copy-start(bf16[2,768]{1,0:T(2,128)(2,1)} %param.8) | copy-start | bytes 9220
  27.9 30.6 %collective-permute-start.1 = (bf16[2,4,2,64,384]{4,3,2,1,0:T(8,128)(2,1)S(1)}, bf16[2,4,2,64,384]{4,3,2,1,0:T(8,128)(2,1)S(1)}, u32[]{:S(2)}, u32[]{:S(2)}) collective-permute-start(bf16[2,4,2,64,384]{4,3,2,1,0:T(8,128)(2,1)S(1)} %pad_maximum_fusion.1), channel_id=1, source_target_pairs={{0,16},{16,32},{32,48},{48,64},{64,80},{80,96},{96,112},{1,17},{17... | collective-permute-start | bytes 2359304 | tf_op jit(solution)/shard_map/ppermute | solution.py:267
  44.0 21.1 %collective-permute-start.2 = (bf16[2,4,2,64,384]{4,3,2,1,0:T(8,128)(2,1)S(1)}, bf16[2,4,2,64,384]{4,3,2,1,0:T(8,128)(2,1)}, u32[]{:S(2)}, u32[]{:S(2)}) collective-permute-start(bf16[2,4,2,64,384]{4,3,2,1,0:T(8,128)(2,1)S(1)} %pad_maximum_fusion.1), channel_id=1, source_target_pairs={{16,0},{32,16},{48,32},{64,48},{80,64},{96,80},{112,96},{17,1},{33... | collective-permute-start | bytes 2359304 | tf_op jit(solution)/shard_map/ppermute | solution.py:267
  45.3 40.7 %collective-permute-start.9 = (bf16[2,4,2,64,384]{4,3,2,1,0:T(8,128)(2,1)S(1)}, bf16[2,4,2,64,384]{4,3,2,1,0:T(8,128)(2,1)S(1)}, u32[]{:S(2)}, u32[]{:S(2)}) collective-permute-start(bf16[2,4,2,64,384]{4,3,2,1,0:T(8,128)(2,1)S(1)} %pad_maximum_fusion.1), channel_id=1, source_target_pairs={{0,8},{8,0},{1,9},{9,1},{2,10},{10,2},{3,11},{11,3},{4,12},{12,4},... | collective-permute-start | bytes 2359304 | tf_op jit(solution)/shard_map/ppermute | solution.py:258
  58.5 7.1 %copy-start.3 = (bf16[2,4,2,64,384]{4,3,2,1,0:T(8,128)(2,1)}, bf16[2,4,2,64,384]{4,3,2,1,0:T(8,128)(2,1)S(1)}, u32[]{:S(2)}) copy-start(bf16[2,4,2,64,384]{4,3,2,1,0:T(8,128)(2,1)S(1)} %collective-permute-done.1.minus) | copy-start | bytes 2359300
  65.1 20.9 %collective-permute-start.10 = (bf16[2,4,2,64,384]{4,3,2,1,0:T(8,128)(2,1)S(1)}, bf16[2,4,2,64,384]{4,3,2,1,0:T(8,128)(2,1)}, u32[]{:S(2)}, u32[]{:S(2)}) collective-permute-start(bf16[2,4,2,64,384]{4,3,2,1,0:T(8,128)(2,1)S(1)} %collective-permute-done.1.minus), channel_id=1, source_target_pairs={{0,8},{8,0},{1,9},{9,1},{2,10},{10,2},{3,11},{11,3},{4,12},{12,4},... | collective-permute-start | bytes 2359304 | tf_op jit(solution)/shard_map/ppermute | solution.py:258
  65.1 20.9 %collective-permute-start.11 = (bf16[2,4,2,64,384]{4,3,2,1,0:T(8,128)(2,1)}, bf16[2,4,2,64,384]{4,3,2,1,0:T(8,128)(2,1)}, u32[]{:S(2)}, u32[]{:S(2)}) collective-permute-start(bf16[2,4,2,64,384]{4,3,2,1,0:T(8,128)(2,1)} %collective-permute-done.2.plus), channel_id=1, source_target_pairs={{0,8},{8,0},{1,9},{9,1},{2,10},{10,2},{3,11},{11,3},{4,12},{12,4},... | collective-permute-start | bytes 2359304 | tf_op jit(solution)/shard_map/ppermute | solution.py:258
  65.6 41.2 %all-to-all-start = ((bf16[128,2,1536]{2,1,0:T(2,128)(2,1)}), bf16[128,2,1536]{2,1,0:T(2,128)(2,1)S(1)}, u32[]{:S(2)}, u32[]{:S(2)}) async-start(bf16[128,2,1536]{2,1,0:T(2,128)(2,1)} %broadcast_in_dim.2), calls=%async_computation | async-start | bytes 1572864 | tf_op jit(solution)/shard_map/all_to_all | solution.py:281
  78.0 30.0 %collective-permute-start.14 = (bf16[1632,128]{1,0:T(8,128)(2,1)}, bf16[1632,128]{1,0:T(8,128)(2,1)}, u32[]{:S(2)}, u32[]{:S(2)}) collective-permute-start(bf16[1632,128]{1,0:T(8,128)(2,1)} %get-tuple-element.21), channel_id=1, source_target_pairs={{0,1},{1,2},{2,3},{3,4},{4,5},{5,6},{6,7},{8,9},{9,10},{10,11},{11... | collective-permute-start | bytes 1253384 | tf_op jit(solution)/shard_map/ppermute | solution.py:280
  81.4 26.6 %collective-permute-start.15 = (bf16[1632,128]{1,0:T(8,128)(2,1)}, bf16[1632,128]{1,0:T(8,128)(2,1)}, u32[]{:S(2)}, u32[]{:S(2)}) collective-permute-start(bf16[1632,128]{1,0:T(8,128)(2,1)} %get-tuple-element.20), channel_id=1, source_target_pairs={{1,0},{2,1},{3,2},{4,3},{5,4},{6,5},{7,6},{9,8},{10,9},{11,10},{12... | collective-permute-start | bytes 1253384 | tf_op jit(solution)/shard_map/ppermute | solution.py:280
  86.0 0.9 copy-start.4
  98.6 19.1 %collective-permute-start.12 = (bf16[1632,128]{1,0:T(8,128)(2,1)}, bf16[1632,128]{1,0:T(8,128)(2,1)S(1)}, u32[]{:S(2)}, u32[]{:S(2)}) collective-permute-start(bf16[1632,128]{1,0:T(8,128)(2,1)} %get-tuple-element.25), channel_id=1, source_target_pairs={{0,1},{1,2},{2,3},{3,4},{4,5},{5,6},{6,7},{8,9},{9,10},{10,11},{11... | collective-permute-start | bytes 1253384 | tf_op jit(solution)/shard_map/ppermute | solution.py:280
  100.5 17.2 %collective-permute-start.13 = (bf16[1632,128]{1,0:T(8,128)(2,1)}, bf16[1632,128]{1,0:T(8,128)(2,1)S(1)}, u32[]{:S(2)}, u32[]{:S(2)}) collective-permute-start(bf16[1632,128]{1,0:T(8,128)(2,1)} %get-tuple-element.26), channel_id=1, source_target_pairs={{1,0},{2,1},{3,2},{4,3},{5,4},{6,5},{7,6},{9,8},{10,9},{11,10},{12... | collective-permute-start | bytes 1253384 | tf_op jit(solution)/shard_map/ppermute | solution.py:280
  117.7 0.8 copy-start.5
  118.5 0.8 copy-start.6
